TPU v7x, 512 devices: a whole 4x8x8 slice. The times are simulated.
512 devices in a mesh: tok: 128 (over y, z_hi, x), tp: 4 (over z_lo, core).
Axes of the slice: x: 4, y: 8, z: 8 (z_hi: 4, z_lo: 2; z = z_hi * 2 + z_lo), core: 2. Of those that a mesh axis runs over, the one named last changes fastest.
Arguments:
- tokens: bfloat16 [131072, 1024], P('tok', 'tp'), may hold values from -6 to 6
- mix_weights: bfloat16 [10, 2, 2, 128, 128], replicated, may hold values from -0.375 to 0.375
- proj_weight: bfloat16 [1024, 2048], P('tp'), may hold values from -0.1875 to 0.1875
- pool_map: int32 [131072], P('tok'), may hold values from 0 to 16383, as said below
- out_cot: bfloat16 [16384, 2048], P('tok', 'tp'), may hold values from -24 to 24
Outputs:
- projected: bfloat16 [16384, 2048], P('tok', 'tp')
- token_grad: bfloat16 [131072, 1024], P('tok', 'tp')
- proj_grad: float32 [2048, 1024], P('tok', 'tp')
Inputs may be any that keep to these rules, and one draw needn't show every extreme that they name: `pool_map`: token t names one of the 128 pooled tokens of its own block of 1024 tokens, numbers (t // 1024) * 128 onward; every pooled token is named by at least one token.
All inputs are finite; a program needn't handle non-finite values.
Results may differ from a plain program's by a relative error of at most 0.017.
Values may be sent and summed in bfloat16 or wider, within the bound.
A program may use at most 64 MiB of HBM per device.

v0:
```python
import math

import jax
import jax.numpy as jnp
from jax import lax
from jax.sharding import Mesh
from jax.sharding import PartitionSpec as P

TOK = ("tok_0", "tok_1", "tok_2")


def split_up(array, dim, count):
    before, after = (array.shape[:dim], array.shape[dim + 1 :])
    return jnp.moveaxis(array.reshape(*before, count, -1, *after), dim, 0)


def sent_and_summed(array, axis, dim):
    count = lax.axis_size(axis)
    blocks = lax.all_to_all(split_up(array, dim, count), axis, 0, 0, tiled=True)
    return jnp.sum(blocks.astype(jnp.float32), axis=0)


def from_everyone(array, axis):
    copies = jnp.broadcast_to(array, (lax.axis_size(axis), *array.shape))
    return lax.all_to_all(copies, axis, split_axis=0, concat_axis=0, tiled=True)


def laid_out(blocks, dim):
    blocks = jnp.moveaxis(blocks, 0, dim)
    dims = blocks.shape
    return blocks.reshape(*dims[:dim], dims[dim] * dims[dim + 1], *dims[dim + 2 :])


def gather_directly(array, axis, dim):
    blocks = from_everyone(array, axis)
    return laid_out(blocks, dim)


def reduced_to_own(blocks, axes, order):
    dims = [lax.axis_size(a) for a in axes]
    blocks = blocks.reshape(*dims, *blocks.shape[1:])
    blocks = blocks.transpose(*order, *range(len(axes), blocks.ndim))
    blocks = blocks.reshape(-1, *blocks.shape[len(axes) :])
    for k in order:
        blocks = lax.psum_scatter(blocks, axes[k], scatter_dimension=0, tiled=True)
    return blocks[0]


def scatter_axes(array, axes, order, dim):
    count = lax.axis_size(axes)
    return reduced_to_own(split_up(array, dim, count), axes, order)


def contract(matrix, operand, backward):
    pattern = "ji,...j->...i" if backward else "ij,...j->...i"
    return jnp.einsum(pattern, matrix, operand, preferred_element_type=jnp.float32)


def local_section(field_now, section_mats, bit_index, backward, block_axis):
    full_shape = field_now.shape
    nblocks = full_shape[block_axis]
    split_shape = (
        full_shape[:block_axis]
        + (nblocks >> bit_index + 1, 2, 1 << bit_index)
        + full_shape[block_axis + 1 :]
    )
    paired = field_now.reshape(split_shape)
    lower_half = lax.index_in_dim(paired, 0, block_axis + 1, keepdims=False)
    upper_half = lax.index_in_dim(paired, 1, block_axis + 1, keepdims=False)
    if backward:
        new_lower = contract(section_mats[0, 0], lower_half, True) + contract(
            section_mats[1, 0], upper_half, True
        )
        new_upper = contract(section_mats[0, 1], lower_half, True) + contract(
            section_mats[1, 1], upper_half, True
        )
    else:
        new_lower = contract(section_mats[0, 0], lower_half, False) + contract(
            section_mats[0, 1], upper_half, False
        )
        new_upper = contract(section_mats[1, 0], lower_half, False) + contract(
            section_mats[1, 1], upper_half, False
        )
    joined = jnp.stack(
        [new_lower.astype(jnp.bfloat16), new_upper.astype(jnp.bfloat16)], axis=block_axis + 1
    )
    return joined.reshape(full_shape)


def mix_tokens(source, mix_weights, section_bits, backward):
    block_rows = mix_weights.shape[-1]
    section_order = list(range(len(section_bits)))
    if backward:
        section_order = section_order[::-1]
    columns = lax.all_to_all(source.T, TOK, split_axis=0, concat_axis=1, tiled=True)
    feat_rows, all_tokens = columns.shape
    field_now = columns.reshape(feat_rows, all_tokens // block_rows, block_rows)
    for section_id in section_order:
        field_now = local_section(
            field_now, mix_weights[section_id], section_bits[section_id], backward, 1
        )
    back_rows = lax.all_to_all(
        field_now.reshape(feat_rows, all_tokens), TOK, split_axis=1, concat_axis=0, tiled=True
    )
    return back_rows.T


def shards(tokens, mix_weights, proj_weight, pool_map, out_cot):
    tok_rows = tokens.shape[0]
    block_rows = mix_weights.shape[-1]
    section_count = mix_weights.shape[0]
    local_blocks = tok_rows // block_rows
    local_bits = local_blocks.bit_length() - 1
    tok_devices = lax.axis_size(TOK)
    all_bits = local_bits + tok_devices.bit_length() - 1
    section_bits = [section_id % all_bits for section_id in range(section_count)]
    mixed = mix_tokens(tokens, mix_weights, section_bits, False)
    pool_rows = out_cot.shape[0]
    local_map = pool_map - lax.axis_index(TOK) * pool_rows
    membership = (local_map[None, :] == jnp.arange(pool_rows, dtype=jnp.int32)[:, None]).astype(
        jnp.bfloat16
    )
    counts = jnp.sum(membership.astype(jnp.float32), axis=1)
    group_sums = jnp.dot(membership, mixed, preferred_element_type=jnp.float32)
    pooled = (group_sums / counts[:, None]).astype(jnp.bfloat16)
    proj_share = sent_and_summed(
        lax.dot_general(
            proj_weight, pooled, (((0,), (1,)), ((), ())), preferred_element_type=jnp.float32
        ).astype(jnp.bfloat16),
        "tp",
        0,
    )
    projected = proj_share.T.astype(jnp.bfloat16)
    cot_full = gather_directly(out_cot, "tp", 1)
    d_pooled = lax.dot_general(
        cot_full, proj_weight, (((1,), (1,)), ((), ())), preferred_element_type=jnp.float32
    )
    back_rows = jnp.take(d_pooled / counts[:, None], local_map, axis=0).astype(jnp.bfloat16)
    token_grad = mix_tokens(back_rows, mix_weights, section_bits, True)
    grad_share = scatter_axes(
        lax.dot_general(
            cot_full, pooled, (((0,), (0,)), ((), ())), preferred_element_type=jnp.float32
        ),
        TOK,
        (0, 2, 1),
        0,
    )
    grad_scale = 1.0 / math.sqrt(pool_rows * tok_devices)
    proj_grad = grad_share * grad_scale
    return (projected, token_grad, proj_grad)


def solution(mesh):
    split = Mesh(mesh.devices.reshape(8, 4, 4, mesh.shape["tp"]), ("tok_0", "tok_1", "tok_2", "tp"))
    return jax.shard_map(
        shards,
        mesh=split,
        in_specs=(P(TOK, "tp"), P(), P("tp", None), P(TOK), P(TOK, "tp")),
        out_specs=(P(TOK, "tp"), P(TOK, "tp"), P(TOK, "tp")),
        check_vma=False,
    )
```

profile of v0, /device:TPU:1, one launch (start us, length us, event | category | flops | bytes accessed | tf_op | source)
XLA Modules:
  0.0 243.9 jit_solution(1172022805628178525)
XLA Ops:
  7.2 1.1 copy.250
  8.3 0.9 broadcast_in_dim.20
  9.2 10.4 %all-to-all-start.3 = ((bf16[4,128,512]{1,2,0:T(8,128)(2,1)}), bf16[4,128,512]{1,2,0:T(8,128)(2,1)S(1)}, u32[]{:S(2)}, u32[]{:S(2)}) async-start(bf16[4,128,512]{1,2,0:T(8,128)(2,1)} %broadcast_in_dim.20), calls=%async_computation.3 | async-start | bytes 1048576 | tf_op jit(solution)/shard_map/all_to_all | solution.py:25
  19.6 1.2 copy.217
  20.9 1.0 all_to_all.58
  21.9 5.6 %all-to-all-done.3 = bf16[4,128,512]{1,2,0:T(8,128)(2,1)S(1)} async-done(((bf16[4,128,512]{1,2,0:T(8,128)(2,1)}), bf16[4,128,512]{1,2,0:T(8,128)(2,1)S(1)}, u32[]{:S(2)}, u32[]{:S(2)}) %all-to-all-start.3) | async-done | bytes 524320 | tf_op jit(solution)/shard_map/all_to_all | solution.py:25
  27.5 14.6 %all-to-all-start = ((bf16[128,2,1024]{2,1,0:T(2,128)(2,1)}), bf16[128,2,1024]{2,1,0:T(2,128)(2,1)S(1)}, u32[]{:S(2)}, u32[]{:S(2)}) async-start(bf16[128,2,1024]{2,1,0:T(2,128)(2,1)} %all_to_all.58), calls=%async_computation | async-start | bytes 1048576 | tf_op jit(solution)/shard_map/all_to_all | solution.py:95
  42.2 1.0 slice_bitcast_fusion.96
  43.3 0.5 convolution_divide_fusion.1
  43.8 3.9 %gather_fusion = bf16[1024,256]{1,0:T(8,128)(2,1)S(1)} fusion(bf16[128,256]{1,0:T(8,128)(2,1)S(1)} %convolution_divide_fusion.1, s32[1024]{0:T(1024)S(1)} %fusion.121), kind=kCustom, calls=%fused_computation | custom fusion | bytes 1052672 | tf_op jit(solution)/shard_map/jit(_take)/gather | solution.py:138
  48.1 1.0 all_to_all.67
  49.2 13.5 %all-to-all-done = bf16[128,2,1024]{2,1,0:T(2,128)(2,1)S(1)} async-done(((bf16[128,2,1024]{2,1,0:T(2,128)(2,1)}), bf16[128,2,1024]{2,1,0:T(2,128)(2,1)S(1)}, u32[]{:S(2)}, u32[]{:S(2)}) %all-to-all-start) | async-done | bytes 524320 | tf_op jit(solution)/shard_map/all_to_all | solution.py:95
  62.6 7.0 %all-to-all-start.4 = ((bf16[128,2,1024]{2,1,0:T(2,128)(2,1)}), bf16[128,2,1024]{2,1,0:T(2,128)(2,1)S(1)}, u32[]{:S(2)}, u32[]{:S(2)}) async-start(bf16[128,2,1024]{2,1,0:T(2,128)(2,1)} %all_to_all.67), calls=%async_computation.4 | async-start | bytes 1048576 | tf_op jit(solution)/shard_map/all_to_all | solution.py:95
  69.7 0.4 reshape_reshape.61
  70.1 0.7 fusion.124
  71.6 0.2 fusion
  73.0 0.9 fusion.123
  74.7 0.2 fusion.72
  75.0 0.4 copy.226
  75.9 0.2 fusion.71
  76.1 0.2 fusion.70
  76.5 0.3 copy-done.6
  77.8 0.3 copy-done.7
  79.2 0.3 copy-done.8
  80.2 0.2 fusion.64
  80.6 0.3 copy-done.9
  81.9 0.3 copy-done.11
  83.3 0.3 copy-done.13
  83.8 0.2 fusion.59
  84.3 0.2 fusion.58
  84.9 1.3 copy.248
  86.2 2.4 all-to-all-done.4
  88.6 13.0 %all-to-all-start.1 = ((bf16[2,128,1024]{2,0,1:T(2,128)(2,1)}), bf16[2,128,1024]{2,0,1:T(2,128)(2,1)S(1)}, u32[]{:S(2)}, u32[]{:S(2)}) async-start(bf16[2,128,1024]{2,0,1:T(2,128)(2,1)} %copy.248), calls=%async_computation.1 | async-start | bytes 1048576 | tf_op jit(solution)/shard_map/all_to_all | solution.py:102
  101.6 0.3 reduce-scatter.4.cloned.1.call-start
  102.2 1.0 fusion.102
  103.2 1.0 fusion.101
  104.2 1.0 fusion.20
  105.2 1.0 fusion.21
  107.2 0.4 copy-done.10
  111.7 0.9 fusion.47
  112.9 0.9 fusion.46
  113.8 6.3 %all-to-all-done.1 = bf16[2,128,1024]{2,0,1:T(2,128)(2,1)S(1)} async-done(((bf16[2,128,1024]{2,0,1:T(2,128)(2,1)}), bf16[2,128,1024]{2,0,1:T(2,128)(2,1)S(1)}, u32[]{:S(2)}, u32[]{:S(2)}) %all-to-all-start.1) | async-done | bytes 524320 | tf_op jit(solution)/shard_map/all_to_all | solution.py:102
  120.3 0.3 fusion.76
  120.7 0.6 copy-done.16
  121.3 1.5 convolution_bitcast_fusion
  122.8 1.8 copy.283
  124.6 3.2 %copy.284 = f32[8,4,4,16,256]{4,3,2,1,0:T(8,128)} copy(f32[8,4,4,16,256]{4,3,1,2,0:T(8,128)} %bitcast.675) | data formatting | bytes 4194304 | tf_op jit(solution)/shard_map/transpose | solution.py:42
  127.8 0.9 copy-done.14
  130.1 0.5 copy.275
  131.6 0.5 copy.278
  133.1 0.5 copy.281
  133.6 0.4 all_to_all.70
  134.0 1.3 copy.282
  135.3 9.3 %all-to-all-start.5 = ((bf16[2,128,1024]{2,0,1:T(2,128)(2,1)}), bf16[2,128,1024]{2,0,1:T(2,128)(2,1)S(1)}, u32[]{:S(2)}, u32[]{:S(2)}) async-start(bf16[2,128,1024]{2,0,1:T(2,128)(2,1)} %copy.282), calls=%async_computation.5 | async-start | bytes 1048576 | tf_op jit(solution)/shard_map/all_to_all | solution.py:102
  144.6 0.3 convolution_convert_fusion
  144.9 0.9 copy.385
  145.8 23.8 %all-to-all-done.5 = bf16[2,128,1024]{2,0,1:T(2,128)(2,1)S(1)} async-done(((bf16[2,128,1024]{2,0,1:T(2,128)(2,1)}), bf16[2,128,1024]{2,0,1:T(2,128)(2,1)S(1)}, u32[]{:S(2)}, u32[]{:S(2)}) %all-to-all-start.5) | async-done | bytes 524320 | tf_op jit(solution)/shard_map/all_to_all | solution.py:102
  169.6 8.5 %all-to-all-start.2 = ((bf16[4,512,128]{1,2,0:T(8,128)(2,1)}), bf16[4,512,128]{1,2,0:T(8,128)(2,1)S(1)}, u32[]{:S(2)}, u32[]{:S(2)}) async-start(bf16[4,512,128]{1,2,0:T(8,128)(2,1)} %bitcast.673), calls=%async_computation.2 | async-start | bytes 1048576 | tf_op jit(solution)/shard_map/all_to_all | solution.py:19
  178.1 0.7 reduce-scatter.6.cloned.1.call-update
  178.9 25.8 %reduce-scatter.6.cloned.1.call-done = f32[4,16,256]{2,1,0:T(8,128)} async-done(((f32[16,16,256]{2,1,0:T(8,128)}), f32[4,16,256]{2,1,0:T(8,128)}) %reduce-scatter.6.cloned.1.call-update) | async-done | bytes 65552 | tf_op jit(solution)/shard_map/reduce_scatter | solution.py:45
  204.9 1.0 copy.285
  205.9 0.7 reduce_sum.22
  206.7 29.4 %reduce-scatter.8.cloned.1.call-done = f32[1,16,256]{2,1,0:T(8,128)} async-done(((f32[4,16,256]{2,1,0:T(8,128)}), f32[1,16,256]{2,1,0:T(8,128)}) %reduce-scatter.8.cloned.1.call-update) | async-done | bytes 16400 | tf_op jit(solution)/shard_map/reduce_scatter | solution.py:45
  236.1 1.3 multiply_bitcast_fusion
  (149 shorter events, 18.4 us)
Async XLA Ops:
  7.2 36.1 %copy-start = (bf16[256,2048]{1,0:T(8,128)(2,1)S(1)}, bf16[256,2048]{1,0:T(8,128)(2,1)}, u32[]{:S(2)}) copy-start(bf16[256,2048]{1,0:T(8,128)(2,1)} %param.7) | copy-start | bytes 3145732
  7.2 14.7 %copy-start.18 = (s32[1024]{0:T(1024)S(1)}, s32[1024]{0:T(1024)}, u32[]{:S(2)}) copy-start(s32[1024]{0:T(1024)} %param.8) | copy-start | bytes 12292
  9.2 33.0 %copy-start.2 = (bf16[10,2,2,128,128]{4,3,2,1,0:T(8,128)(2,1)S(1)}, bf16[10,2,2,128,128]{4,3,2,1,0:T(8,128)(2,1)}, u32[]{:S(2)}) copy-start(bf16[10,2,2,128,128]{4,3,2,1,0:T(8,128)(2,1)} %param.6) | copy-start | bytes 3932164
  9.2 18.3 %all-to-all-start.3 = ((bf16[4,128,512]{1,2,0:T(8,128)(2,1)}), bf16[4,128,512]{1,2,0:T(8,128)(2,1)S(1)}, u32[]{:S(2)}, u32[]{:S(2)}) async-start(bf16[4,128,512]{1,2,0:T(8,128)(2,1)} %broadcast_in_dim.20), calls=%async_computation.3 | async-start | bytes 1048576 | tf_op jit(solution)/shard_map/all_to_all | solution.py:25
  27.5 16.3 %copy-start.1 = (bf16[4,128,512]{1,2,0:T(8,128)(2,1)}, bf16[4,128,512]{1,2,0:T(8,128)(2,1)S(1)}, u32[]{:S(2)}) copy-start(bf16[4,128,512]{1,2,0:T(8,128)(2,1)S(1)} %all-to-all-done.3) | copy-start | bytes 1572868
  27.5 35.2 %all-to-all-start = ((bf16[128,2,1024]{2,1,0:T(2,128)(2,1)}), bf16[128,2,1024]{2,1,0:T(2,128)(2,1)S(1)}, u32[]{:S(2)}, u32[]{:S(2)}) async-start(bf16[128,2,1024]{2,1,0:T(2,128)(2,1)} %all_to_all.58), calls=%async_computation | async-start | bytes 1048576 | tf_op jit(solution)/shard_map/all_to_all | solution.py:95
  62.6 26.0 %all-to-all-start.4 = ((bf16[128,2,1024]{2,1,0:T(2,128)(2,1)}), bf16[128,2,1024]{2,1,0:T(2,128)(2,1)S(1)}, u32[]{:S(2)}, u32[]{:S(2)}) async-start(bf16[128,2,1024]{2,1,0:T(2,128)(2,1)} %all_to_all.67), calls=%async_computation.4 | async-start | bytes 1048576 | tf_op jit(solution)/shard_map/all_to_all | solution.py:95
  71.1 0.9 copy-start.3
  72.9 1.1 copy-start.4
  74.5 1.0 copy-start.5
  75.9 0.9 copy-start.6
  77.3 0.9 copy-start.7
  78.6 0.9 copy-start.8
  80.0 0.9 copy-start.9
  81.4 0.9 copy-start.11
  82.7 0.9 copy-start.13
  88.6 31.6 %all-to-all-start.1 = ((bf16[2,128,1024]{2,0,1:T(2,128)(2,1)}), bf16[2,128,1024]{2,0,1:T(2,128)(2,1)S(1)}, u32[]{:S(2)}, u32[]{:S(2)}) async-start(bf16[2,128,1024]{2,0,1:T(2,128)(2,1)} %copy.248), calls=%async_computation.1 | async-start | bytes 1048576 | tf_op jit(solution)/shard_map/all_to_all | solution.py:102
  101.6 76.5 %reduce-scatter.4.cloned.1.call-start = ((), (), s32[]{:S(2)}) async-start(), calls=%async_computation.9 | async-start | bytes 2359296 | tf_op jit(solution)/shard_map/reduce_scatter | solution.py:45
  103.2 3.0 %copy-start.12 = (bf16[2,2,128,128]{3,2,1,0:T(8,128)(2,1)S(1)}, bf16[2,2,128,128]{3,2,1,0:T(8,128)(2,1)}, u32[]{:S(2)}) copy-start(bf16[2,2,128,128]{3,2,1,0:T(8,128)(2,1)} %get-tuple-element.26) | copy-start | bytes 393220
  106.7 0.9 copy-start.10
  120.7 0.6 copy-start.16
  127.8 0.9 copy-start.14
  127.8 1.0 copy-start.15
  133.0 11.5 %copy-start.17 = (bf16[128,256]{1,0:T(8,128)(2,1)S(1)}, bf16[128,256]{1,0:T(8,128)(2,1)}, u32[]{:S(2)}) copy-start(bf16[128,256]{1,0:T(8,128)(2,1)} %copy-done.16) | copy-start | bytes 196612
  135.3 34.3 %all-to-all-start.5 = ((bf16[2,128,1024]{2,0,1:T(2,128)(2,1)}), bf16[2,128,1024]{2,0,1:T(2,128)(2,1)S(1)}, u32[]{:S(2)}, u32[]{:S(2)}) async-start(bf16[2,128,1024]{2,0,1:T(2,128)(2,1)} %copy.282), calls=%async_computation.5 | async-start | bytes 1048576 | tf_op jit(solution)/shard_map/all_to_all | solution.py:102
  169.6 36.4 %all-to-all-start.2 = ((bf16[4,512,128]{1,2,0:T(8,128)(2,1)}), bf16[4,512,128]{1,2,0:T(8,128)(2,1)S(1)}, u32[]{:S(2)}, u32[]{:S(2)}) async-start(bf16[4,512,128]{1,2,0:T(8,128)(2,1)} %bitcast.673), calls=%async_computation.2 | async-start | bytes 1048576 | tf_op jit(solution)/shard_map/all_to_all | solution.py:19
  178.1 26.6 %reduce-scatter.6.cloned.1.call-start = ((), (), s32[]{:S(2)}) async-start(), calls=%async_computation.10 | async-start | bytes 327680 | tf_op jit(solution)/shard_map/reduce_scatter | solution.py:45
  178.8 57.2 %reduce-scatter.8.cloned.1.call-start = ((), (), s32[]{:S(2)}) async-start(), calls=%async_computation.11 | async-start | bytes 81920 | tf_op jit(solution)/shard_map/reduce_scatter | solution.py:45
Sparse Core Ops, SparseCore 0:
  127.9 47.1 reduce-scatter.3
  181.7 22.9 reduce-scatter.5
  207.5 28.5 reduce-scatter.7
where the time goes:
time: 246 us; the launch traced here: 244 us
  waiting for transfers between devices  108 us (44%)
  starting transfers between devices  63.1 us (26%)
  local copies, waits for them, and re-layouts  30.4 us (12%)
  matrix products  24.6 us (10%)
  between operations  14.9 us (6%)
  other arithmetic  3.4 us (1%)
    reduce_scatter x3, waiting for transfers between devices, reduced_to_own(): blocks = lax.psum_scatter(blocks, axes[k], scatter_dimension=0, tiled=True)  55.2 us
    all_to_all x2, waiting for transfers between devices, mix_tokens(): lax.all_to_all(field_now.reshape(feat_rows, all_tokens), TOK, split_axis=...  30.1 us
    all_to_all x2, starting transfers between devices, mix_tokens(): lax.all_to_all(field_now.reshape(feat_rows, all_tokens), TOK, split_axis=...  22.3 us
    dot_general x80, matrix products, contract(): jnp.einsum(pattern, matrix, operand, preferred_element_type=jnp.float32)  22 us
    all_to_all x2, starting transfers between devices, mix_tokens(): lax.all_to_all(source.T, TOK, split_axis=0, concat_axis=1, tiled=True)  21.6 us
    all_to_all x2, waiting for transfers between devices, mix_tokens(): lax.all_to_all(source.T, TOK, split_axis=0, concat_axis=1, tiled=True)  15.8 us
    all_to_all x1, starting transfers between devices, from_everyone(): return lax.all_to_all(copies, axis, split_axis=0, concat_axis=0, tiled=True)  10.4 us
    all_to_all x1, starting transfers between devices, sent_and_summed(): blocks = lax.all_to_all(split_up(array, dim, count), axis, 0, 0, tiled=True)  8.51 us
  transfers between devices with their start and end apart: 9, of which 7 were waited for; matrix products, arithmetic and copies ran while one was open for 17% of the time, Pallas kernels for 0%

commit v1 on v0

v1 whole, which is shorter than its diff:
```python
import functools
import math

import jax
import jax.numpy as jnp
from jax import lax
from jax.experimental import pallas as pl
from jax.experimental.pallas import tpu as pltpu
from jax.sharding import PartitionSpec as P

MESH = pl.DeviceIdType.MESH
BLK = 128
NX = 4
NN = (((1,), (0,)), ((), ()))
NT = (((1,), (1,)), ((), ()))
F_IN, F_OUT, B_IN, B_OUT, COT, COTX, POOLX, PROJ, GRAD = range(9)


def mm(a, b, dims):
    return lax.dot_general(a, b, dims, preferred_element_type=jnp.float32)


def section_matrix(mixw, s):
    top = jnp.concatenate([mixw[s, 0, 0], mixw[s, 0, 1]], axis=1)
    low = jnp.concatenate([mixw[s, 1, 0], mixw[s, 1, 1]], axis=1)
    return jnp.concatenate([top, low], axis=0)


def wait_bytes(sem, ref):
    pltpu.make_async_copy(ref, ref, sem).wait()


def kernel(
    nt, ntp, tokens, mixw, pw, pmap, cot, projected, token_grad, proj_grad,
    xs, yt, xr, gs, ut, vt, onehot, cf, cx, pool, px, ps, pr, cs, cr, send, recv,
):
    me = lax.axis_index("tok")
    mytp = lax.axis_index("tp")
    feats = tokens.shape[1]
    blocks = tokens.shape[0] // BLK
    groups = nt // blocks
    frows = feats // groups
    npool = cot.shape[0]
    equart = cot.shape[1]
    others = nt // NX
    mex, mehi = lax.rem(me, NX), lax.div(me, NX)

    barrier = pltpu.get_barrier_semaphore()

    def greet(i, c):
        pl.semaphore_signal(barrier, inc=1, device_id={"tok": lax.rem(me + i, nt)}, device_id_type=MESH)
        return c

    lax.fori_loop(1, nt, greet, 0)
    for i in range(1, ntp):
        pl.semaphore_signal(barrier, inc=1, device_id={"tp": lax.rem(mytp + i, ntp)}, device_id_type=MESH)

    def exchange(kind, src, dst):
        def one(i, c):
            d = lax.rem(me + i, nt)
            pltpu.make_async_remote_copy(
                src_ref=src.at[d], dst_ref=dst.at[me], send_sem=send.at[kind], recv_sem=recv.at[kind],
                device_id={"tok": d}, device_id_type=MESH,
            ).start()
            return c

        pltpu.make_async_copy(src.at[me], dst.at[me], recv.at[kind]).start()
        lax.fori_loop(1, nt, one, 0)

    def load_block(ref, j):
        parts = [ref[g * blocks + j] for g in range(groups)]
        return jnp.concatenate(parts, axis=0) if groups > 1 else parts[0]

    def store_block(ref, j, value):
        for g in range(groups):
            ref[g * blocks + j] = value[g * frows : (g + 1) * frows]

    def local_pairs(bit):
        return [(j, j | (1 << bit)) for j in range(blocks) if not j & (1 << bit)]

    cf[mytp] = cot[...].astype(jnp.float32).T.astype(jnp.bfloat16)

    w = section_matrix(mixw, 0)
    for lo, hi in local_pairs(0):
        out = mm(w, tokens[lo * BLK : (hi + 1) * BLK], NN).T.astype(jnp.bfloat16)
        store_block(xs, lo, out[:, :BLK])
        store_block(xs, hi, out[:, BLK:])
    for bit in (1, 2):
        w = section_matrix(mixw, bit)
        for lo, hi in local_pairs(bit):
            pair = jnp.concatenate([load_block(xs, lo), load_block(xs, hi)], axis=1)
            out = mm(pair, w, NT).astype(jnp.bfloat16)
            store_block(xs, lo, out[:, :BLK])
            store_block(xs, hi, out[:, BLK:])

    pl.semaphore_wait(barrier, nt - 1 + ntp - 1)

    for i in range(1, ntp):
        d = lax.rem(mytp + i, ntp)
        pltpu.make_async_remote_copy(
            src_ref=cf.at[mytp], dst_ref=cf.at[mytp], send_sem=send.at[COT], recv_sem=recv.at[COT],
            device_id={"tp": d}, device_id_type=MESH,
        ).start()
    exchange(F_IN, xs, yt)

    pid = lax.broadcasted_iota(jnp.int32, (npool, BLK), 0) + me * npool
    for j in range(blocks):
        hit = pid == jnp.broadcast_to(pmap[j : j + 1, :], (npool, BLK))
        onehot[:, j * BLK : (j + 1) * BLK] = jnp.where(hit, 1.0, 0.0).astype(jnp.bfloat16)
    ones = jnp.ones((8, blocks * BLK), jnp.bfloat16)
    counts_row = mm(ones, onehot[...], NT)[0:1]
    counts_col = jnp.sum(onehot[...].astype(jnp.float32), axis=1, keepdims=True)

    wait_bytes(recv.at[COT], cf.at[pl.ds(0, ntp - 1)])
    dp = mm(pw[:, 0:equart], cf[0], NN)
    for i in range(1, ntp):
        dp = dp + mm(pw[:, i * equart : (i + 1) * equart], cf[i], NN)
    dp = (dp / counts_row).astype(jnp.bfloat16)
    for j in range(blocks):
        store_block(gs, j, mm(dp, onehot[:, j * BLK : (j + 1) * BLK], NN).astype(jnp.bfloat16))
    exchange(B_IN, gs, ut)

    for i in range(NX):
        dx = lax.rem(mex + i, NX)
        if i == 0:
            pltpu.make_async_copy(cf.at[dx], cx.at[mex], recv.at[COTX]).start()
        else:
            pltpu.make_async_remote_copy(
                src_ref=cf.at[dx], dst_ref=cx.at[mex], send_sem=send.at[COTX], recv_sem=recv.at[COTX],
                device_id={"tok": mehi * NX + dx}, device_id_type=MESH,
            ).start()

    def across(ref, bit, s, dims):
        w = section_matrix(mixw, s)
        stride = 1 << bit
        half = nt // 2
        run = min(16, half)

        def body(c, carry):
            if stride >= run:
                p = c * run
                lo = (p // stride) * (2 * stride) + p % stride
                lo = pl.multiple_of(lo, run)
                a = ref[pl.ds(lo, run)].reshape(run * frows, BLK)
                b = ref[pl.ds(lo + stride, run)].reshape(run * frows, BLK)
                out = mm(jnp.concatenate([a, b], axis=1), w, dims).astype(jnp.bfloat16)
                ref[pl.ds(lo, run)] = out[:, :BLK].reshape(run, frows, BLK)
                ref[pl.ds(lo + stride, run)] = out[:, BLK:].reshape(run, frows, BLK)
            else:
                base = c * 2 * run
                v = ref[pl.ds(base, 2 * run)].reshape(run // stride, 2, stride, frows, BLK)
                a = v[:, 0].reshape(run * frows, BLK)
                b = v[:, 1].reshape(run * frows, BLK)
                out = mm(jnp.concatenate([a, b], axis=1), w, dims).astype(jnp.bfloat16)
                a = out[:, :BLK].reshape(run // stride, 1, stride, frows, BLK)
                b = out[:, BLK:].reshape(run // stride, 1, stride, frows, BLK)
                ref[pl.ds(base, 2 * run)] = jnp.concatenate([a, b], axis=1).reshape(2 * run, frows, BLK)
            return carry

        lax.fori_loop(0, half // run, body, 0)

    bits = nt.bit_length() - 1
    wait_bytes(recv.at[F_IN], yt)
    for bit in range(bits):
        across(yt, bit, 3 + bit, NT)
    exchange(F_OUT, yt, xr)

    wait_bytes(recv.at[B_IN], ut)
    for bit in reversed(range(bits)):
        across(ut, bit, 3 + bit, NN)
    exchange(B_OUT, ut, vt)

    wait_bytes(recv.at[F_OUT], xr)
    total = mm(onehot[:, 0:BLK], load_block(xr, 0), NT)
    for j in range(1, blocks):
        total = total + mm(onehot[:, j * BLK : (j + 1) * BLK], load_block(xr, j), NT)
    pool[...] = (total / counts_col).astype(jnp.bfloat16)
    for i in range(NX):
        dx = lax.rem(mex + i, NX)
        if i == 0:
            pltpu.make_async_copy(pool, px.at[mex], recv.at[POOLX]).start()
        else:
            pltpu.make_async_remote_copy(
                src_ref=pool, dst_ref=px.at[mex], send_sem=send.at[POOLX], recv_sem=recv.at[POOLX],
                device_id={"tok": mehi * NX + dx}, device_id_type=MESH,
            ).start()
    for i in range(ntp):
        ps[i] = mm(pool[...], pw[:, i * equart : (i + 1) * equart], NN).astype(jnp.bfloat16)
    pltpu.make_async_copy(ps.at[mytp], pr.at[mytp], recv.at[PROJ]).start()
    for i in range(1, ntp):
        d = lax.rem(mytp + i, ntp)
        pltpu.make_async_remote_copy(
            src_ref=ps.at[d], dst_ref=pr.at[mytp], send_sem=send.at[PROJ], recv_sem=recv.at[PROJ],
            device_id={"tp": d}, device_id_type=MESH,
        ).start()

    wait_bytes(recv.at[COTX], cx)
    wait_bytes(recv.at[POOLX], px)
    erows = equart // others
    parts = min(4, others)
    half = equart // parts
    for r in range(parts):
        part = mm(cx[0, r * half : (r + 1) * half], px[0], NN)
        for i in range(1, NX):
            part = part + mm(cx[i, r * half : (r + 1) * half], px[i], NN)
        n = others // parts
        cs[r * n : (r + 1) * n] = part.astype(jnp.bfloat16).reshape(n, erows, feats)

    def give(i, c):
        b = lax.rem(mehi + i, others)
        d = mex * others + b

        @pl.when(d == me)
        def _():
            pltpu.make_async_copy(cs.at[b], cr.at[mehi], recv.at[GRAD]).start()

        @pl.when(d != me)
        def _():
            pltpu.make_async_remote_copy(
                src_ref=cs.at[b], dst_ref=cr.at[mehi], send_sem=send.at[GRAD], recv_sem=recv.at[GRAD],
                device_id={"tok": d}, device_id_type=MESH,
            ).start()

        return c

    lax.fori_loop(0, others, give, 0)

    wait_bytes(recv.at[B_OUT], vt)
    for bit in (2, 1):
        w = section_matrix(mixw, bit)
        for lo, hi in local_pairs(bit):
            pair = jnp.concatenate([load_block(vt, lo), load_block(vt, hi)], axis=1)
            out = mm(pair, w, NN).astype(jnp.bfloat16)
            store_block(vt, lo, out[:, :BLK])
            store_block(vt, hi, out[:, BLK:])
    w = section_matrix(mixw, 0)
    for lo, hi in local_pairs(0):
        pair = jnp.concatenate([load_block(vt, lo), load_block(vt, hi)], axis=1)
        token_grad[lo * BLK : (hi + 1) * BLK] = mm(pair, w, NN).T.astype(jnp.bfloat16)

    wait_bytes(recv.at[PROJ], pr)
    proj = pr[0].astype(jnp.float32)
    for i in range(1, ntp):
        proj = proj + pr[i].astype(jnp.float32)
    projected[...] = proj.astype(jnp.bfloat16)

    wait_bytes(recv.at[GRAD], cr)
    proj_grad[...] = jnp.sum(cr[...].astype(jnp.float32), axis=0) * (1.0 / math.sqrt(npool * nt))

    for kind, ref in ((F_IN, yt), (B_IN, ut), (F_OUT, xr), (B_OUT, vt)):
        wait_bytes(send.at[kind], ref.at[pl.ds(0, nt - 1)])
    wait_bytes(send.at[COT], cf.at[pl.ds(0, ntp - 1)])
    wait_bytes(send.at[PROJ], pr.at[pl.ds(0, ntp - 1)])
    wait_bytes(send.at[COTX], cx.at[pl.ds(0, NX - 1)])
    wait_bytes(send.at[POOLX], px.at[pl.ds(0, NX - 1)])
    mine = lax.div(me, others) == mex

    @pl.when(mine)
    def _():
        wait_bytes(send.at[GRAD], cr.at[pl.ds(0, others - 1)])

    @pl.when(jnp.logical_not(mine))
    def _():
        wait_bytes(send.at[GRAD], cr)


def shards(nt, ntp, tokens, mixw, pw, pool_map, cot):
    rows, feats = tokens.shape
    blocks = rows // BLK
    frows = feats * blocks // nt
    npool, equart = cot.shape
    others = nt // NX
    erows = equart // others
    bf = jnp.bfloat16
    tiles = pltpu.VMEM((nt, frows, BLK), bf)
    vmem = pl.BlockSpec(memory_space=pltpu.VMEM)
    return pl.pallas_call(
        functools.partial(kernel, nt, ntp),
        out_shape=(
            jax.ShapeDtypeStruct((npool, equart), bf),
            jax.ShapeDtypeStruct((rows, feats), bf),
            jax.ShapeDtypeStruct((erows, feats), jnp.float32),
        ),
        in_specs=[vmem] * 5,
        out_specs=(vmem,) * 3,
        scratch_shapes=[
            tiles, tiles, tiles, tiles, tiles, tiles,
            pltpu.VMEM((npool, rows), bf),
            pltpu.VMEM((ntp, equart, npool), bf),
            pltpu.VMEM((NX, equart, npool), bf),
            pltpu.VMEM((npool, feats), bf),
            pltpu.VMEM((NX, npool, feats), bf),
            pltpu.VMEM((ntp, npool, equart), bf),
            pltpu.VMEM((ntp, npool, equart), bf),
            pltpu.VMEM((others, erows, feats), bf),
            pltpu.VMEM((others, erows, feats), bf),
            pltpu.SemaphoreType.DMA((9,)),
            pltpu.SemaphoreType.DMA((9,)),
        ],
        compiler_params=pltpu.CompilerParams(collective_id=0, has_side_effects=True),
    )(tokens, mixw, pw, pool_map.reshape(blocks, BLK), cot)


def solution(mesh):
    nt, ntp = mesh.shape["tok"], mesh.shape["tp"]
    return jax.shard_map(
        functools.partial(shards, nt, ntp),
        mesh=mesh,
        in_specs=(P("tok", "tp"), P(), P("tp", None), P("tok"), P("tok", "tp")),
        out_specs=(P("tok", "tp"), P("tok", "tp"), P("tok", "tp")),
        check_vma=False,
    )
```

time: 246 us -> 115 us (0.47)
  Pallas kernels: 0 us -> 110 us
  waiting for transfers between devices: 108 us -> 0 us
  starting transfers between devices: 63.1 us -> 0 us
  local copies, waits for them, and re-layouts: 30.4 us -> 4.05 us
  matrix products: 24.6 us -> 0 us
  between operations: 14.9 us -> 0.65 us
  other arithmetic: 3.4 us -> 0 us
    pallas_call x0 -> x1, Pallas kernels: none -> 110 us  [shards(): pl.pallas_call(functools.partial(kernel, nt, ntp), out_shape=(jax.ShapeDt...]
    all_to_all x6 -> x0, starting transfers between devices: 62.8 us -> none  [the longest x2 22.3 us: mix_tokens(): lax.all_to_all(field_now.reshape(feat_rows, all_tokens), TOK, split_axis=...]
    reduce_scatter x3 -> x0, waiting for transfers between devices: 55.2 us -> none  [reduced_to_own(): blocks = lax.psum_scatter(blocks, axes[k], scatter_dimension=0, tiled=True)]
    all_to_all x6 -> x0, waiting for transfers between devices: 51.6 us -> none  [the longest x2 30.1 us: mix_tokens(): lax.all_to_all(field_now.reshape(feat_rows, all_tokens), TOK, split_axis=...]
    dot_general x84 -> x0, matrix products: 24.6 us -> none  [the longest x80 22 us: contract(): jnp.einsum(pattern, matrix, operand, preferred_element_type=jnp.float32)]
    all_to_all x10 -> x0, local copies, waits for them, and re-layouts: 5.88 us -> none  [the longest x6 3.65 us: mix_tokens(): lax.all_to_all(field_now.reshape(feat_rows, all_tokens), TOK, split_axis=...]
    transpose x2 -> x0, local copies, waits for them, and re-layouts: 4.43 us -> none  [the longest x1 3.18 us: reduced_to_own(): blocks = blocks.transpose(*order, *range(len(axes), blocks.ndim))]
    gather x1 -> x0, local copies, waits for them, and re-layouts: 3.94 us -> none  [shards(): jnp.take(d_pooled / counts[:, None], local_map, axis=0).astype(jnp.bfloat16)]
  transfers between devices with their start and end apart: 9 -> 0, of which waited for: 7 -> 0; matrix products, arithmetic and copies ran while one was open for 17% -> 0% of each run, Pallas kernels for 0% -> 0%
where the time goes in v1:
time: 115 us
  Pallas kernels  110 us (96%)
  local copies, waits for them, and re-layouts  4.05 us (4%)
    pallas_call x1, Pallas kernels, shards(): pl.pallas_call(functools.partial(kernel, nt, ntp), out_shape=(jax.ShapeDt...  110 us
    unnamed x5, local copies, waits for them, and re-layouts  4.05 us

profile of v1, /device:TPU:1, one launch (start us, length us, event | category | flops | bytes accessed | tf_op | source)
XLA Modules:
  0.0 114.8 jit_solution(8257528967051872296)
XLA Ops:
  0.6 110.1 %shard_map.76 = (bf16[128,512]{1,0:T(8,128)(2,1)}, bf16[1024,256]{1,0:T(8,128)(2,1)}, f32[16,256]{1,0:T(8,128)}) custom-call(bf16[1024,256]{1,0:T(8,128)(2,1)} %tokens.1, bf16[10,2,2,128,128]{4,3,2,1,0:T(8,128)(2,1)} %mixw.1, bf16[256,2048]{1,0:T(8,128)(2,1)} %pw.1, s32[8,128]{1,0:T(8,128)} %bitcast.1, bf16[128,512]{1,0:T(8,128)(2,1)} %cot.1), custom_call_target="tpu_custom_call" | custom-call | tf_op jit(solution)/shard_map/pallas_call | solution.py:277
  110.8 0.0 copy-start
  110.8 1.6 %copy.11 = bf16[128,512]{1,0:T(8,128)(2,1)} copy(bf16[128,512]{1,0:T(8,128)(2,1)} %get-tuple-element.6) | data formatting | bytes 262144
  112.4 1.9 %copy.12 = bf16[1024,256]{1,0:T(8,128)(2,1)} copy(bf16[1024,256]{1,0:T(8,128)(2,1)} %get-tuple-element.7) | data formatting | bytes 1048576
  114.2 0.0 copy-done
  114.2 0.6 copy.13
Async XLA Ops:
  110.8 3.5 %copy-start = (f32[16,256]{1,0:T(8,128)S(1)}, f32[16,256]{1,0:T(8,128)}, u32[]{:S(2)}) copy-start(f32[16,256]{1,0:T(8,128)} %get-tuple-element.8) | copy-start | bytes 49156

commit v2 on v1

--- a/solution.py
+++ b/solution.py
@@ -13,7 +13,7 @@
 NX = 4
 NN = (((1,), (0,)), ((), ()))
 NT = (((1,), (1,)), ((), ()))
-F_IN, F_OUT, B_IN, B_OUT, COT, COTX, POOLX, PROJ, GRAD = range(9)
+F_IN, F_OUT, B_IN, B_OUT, COT, COTX, POOLX, PROJ, GRAD, COTZ, PROJZ = range(11)
 
 
 def mm(a, b, dims):
@@ -31,8 +31,8 @@
 
 
 def kernel(
-    nt, ntp, tokens, mixw, pw, pmap, cot, projected, token_grad, proj_grad,
-    xs, yt, xr, gs, ut, vt, onehot, cf, cx, pool, px, ps, pr, cs, cr, send, recv,
+    nt, ntp, ny, tokens, mixw, pw, pmap, cot, projected, token_grad, proj_grad,
+    xs, yt, xr, gs, ut, vt, onehot, cf, cx, pool, px, ps, pr, cs, cr, send, recv, ready,
 ):
     me = lax.axis_index("tok")
     mytp = lax.axis_index("tp")
@@ -46,12 +46,21 @@
     mex, mehi = lax.rem(me, NX), lax.div(me, NX)
 
     barrier = pltpu.get_barrier_semaphore()
+    plane = nt // ny
+    myy, myp = lax.div(me, plane), lax.rem(me, plane)
 
     def greet(i, c):
-        pl.semaphore_signal(barrier, inc=1, device_id={"tok": lax.rem(me + i, nt)}, device_id_type=MESH)
+        d = myy * plane + lax.rem(myp + i, plane)
+        pl.semaphore_signal(barrier, inc=1, device_id={"tok": d}, device_id_type=MESH)
         return c
 
-    lax.fori_loop(1, nt, greet, 0)
+    def greet_line(i, c):
+        d = lax.rem(myy + i, ny) * plane + myp
+        pl.semaphore_signal(barrier, inc=1, device_id={"tok": d}, device_id_type=MESH)
+        return c
+
+    lax.fori_loop(1, plane, greet, 0)
+    lax.fori_loop(1, ny, greet_line, 0)
     for i in range(1, ntp):
         pl.semaphore_signal(barrier, inc=1, device_id={"tp": lax.rem(mytp + i, ntp)}, device_id_type=MESH)
 
@@ -66,6 +75,12 @@
 
         pltpu.make_async_copy(src.at[me], dst.at[me], recv.at[kind]).start()
         lax.fori_loop(1, nt, one, 0)
+
+    def remote(src, dst, kind, **to):
+        return pltpu.make_async_remote_copy(
+            src_ref=src, dst_ref=dst, send_sem=send.at[kind], recv_sem=recv.at[kind],
+            device_id=to, device_id_type=MESH,
+        )
 
     def load_block(ref, j):
         parts = [ref[g * blocks + j] for g in range(groups)]
@@ -93,15 +108,31 @@
             store_block(xs, lo, out[:, :BLK])
             store_block(xs, hi, out[:, BLK:])
 
-    pl.semaphore_wait(barrier, nt - 1 + ntp - 1)
-
-    for i in range(1, ntp):
-        d = lax.rem(mytp + i, ntp)
-        pltpu.make_async_remote_copy(
-            src_ref=cf.at[mytp], dst_ref=cf.at[mytp], send_sem=send.at[COT], recv_sem=recv.at[COT],
-            device_id={"tp": d}, device_id_type=MESH,
-        ).start()
-    exchange(F_IN, xs, yt)
+    pl.semaphore_wait(barrier, plane - 1 + ny - 1 + ntp - 1)
+
+    def announce(i, c):
+        d = lax.rem(myy + i, ny) * plane + myp
+        pl.semaphore_signal(ready.at[myy], inc=1, device_id={"tok": d}, device_id_type=MESH)
+        return c
+
+    lax.fori_loop(1, ny, announce, 0)
+    mate, across_z, diagonal = mytp ^ 1, mytp ^ 2, mytp ^ 3
+    remote(cf.at[mytp], cf.at[mytp], COTZ, tp=across_z).start()
+    remote(cf.at[mytp], cf.at[mytp], COT, tp=mate).start()
+
+    pltpu.make_async_copy(xs.at[me], yt.at[me], recv.at[F_IN]).start()
+    for k in range(ny):
+        step = (k + 1) // 2 if k % 2 else ny - k // 2
+        y = lax.rem(myy + step, ny)
+        if k > 0:
+            pl.semaphore_wait(ready.at[y], 1)
+
+        def to_plane(i, c, y=y):
+            d = y * plane + lax.rem(myp + i, plane)
+            remote(xs.at[d], yt.at[me], F_IN, tok=d).start()
+            return c
+
+        lax.fori_loop(1 if k == 0 else 0, plane, to_plane, 0)
 
     pid = lax.broadcasted_iota(jnp.int32, (npool, BLK), 0) + me * npool
     for j in range(blocks):
@@ -111,7 +142,9 @@
     counts_row = mm(ones, onehot[...], NT)[0:1]
     counts_col = jnp.sum(onehot[...].astype(jnp.float32), axis=1, keepdims=True)
 
-    wait_bytes(recv.at[COT], cf.at[pl.ds(0, ntp - 1)])
+    wait_bytes(recv.at[COTZ], cf.at[0])
+    remote(cf.at[across_z], cf.at[across_z], COT, tp=mate).start()
+    wait_bytes(recv.at[COT], cf.at[pl.ds(0, 2)])
     dp = mm(pw[:, 0:equart], cf[0], NN)
     for i in range(1, ntp):
         dp = dp + mm(pw[:, i * equart : (i + 1) * equart], cf[i], NN)
@@ -136,28 +169,24 @@
         half = nt // 2
         run = min(16, half)
 
-        def body(c, carry):
+        for c in range(half // run):
             if stride >= run:
                 p = c * run
                 lo = (p // stride) * (2 * stride) + p % stride
-                lo = pl.multiple_of(lo, run)
-                a = ref[pl.ds(lo, run)].reshape(run * frows, BLK)
-                b = ref[pl.ds(lo + stride, run)].reshape(run * frows, BLK)
+                a = ref[lo : lo + run].reshape(run * frows, BLK)
+                b = ref[lo + stride : lo + stride + run].reshape(run * frows, BLK)
                 out = mm(jnp.concatenate([a, b], axis=1), w, dims).astype(jnp.bfloat16)
-                ref[pl.ds(lo, run)] = out[:, :BLK].reshape(run, frows, BLK)
-                ref[pl.ds(lo + stride, run)] = out[:, BLK:].reshape(run, frows, BLK)
+                ref[lo : lo + run] = out[:, :BLK].reshape(run, frows, BLK)
+                ref[lo + stride : lo + stride + run] = out[:, BLK:].reshape(run, frows, BLK)
             else:
                 base = c * 2 * run
-                v = ref[pl.ds(base, 2 * run)].reshape(run // stride, 2, stride, frows, BLK)
+                v = ref[base : base + 2 * run].reshape(run // stride, 2, stride, frows, BLK)
                 a = v[:, 0].reshape(run * frows, BLK)
                 b = v[:, 1].reshape(run * frows, BLK)
                 out = mm(jnp.concatenate([a, b], axis=1), w, dims).astype(jnp.bfloat16)
                 a = out[:, :BLK].reshape(run // stride, 1, stride, frows, BLK)
                 b = out[:, BLK:].reshape(run // stride, 1, stride, frows, BLK)
-                ref[pl.ds(base, 2 * run)] = jnp.concatenate([a, b], axis=1).reshape(2 * run, frows, BLK)
-            return carry
-
-        lax.fori_loop(0, half // run, body, 0)
+                ref[base : base + 2 * run] = jnp.concatenate([a, b], axis=1).reshape(2 * run, frows, BLK)
 
     bits = nt.bit_length() - 1
     wait_bytes(recv.at[F_IN], yt)
@@ -186,13 +215,8 @@
             ).start()
     for i in range(ntp):
         ps[i] = mm(pool[...], pw[:, i * equart : (i + 1) * equart], NN).astype(jnp.bfloat16)
-    pltpu.make_async_copy(ps.at[mytp], pr.at[mytp], recv.at[PROJ]).start()
-    for i in range(1, ntp):
-        d = lax.rem(mytp + i, ntp)
-        pltpu.make_async_remote_copy(
-            src_ref=ps.at[d], dst_ref=pr.at[mytp], send_sem=send.at[PROJ], recv_sem=recv.at[PROJ],
-            device_id={"tp": d}, device_id_type=MESH,
-        ).start()
+    remote(ps.at[mate], pr.at[0], PROJ, tp=mate).start()
+    remote(ps.at[diagonal], pr.at[1], PROJ, tp=mate).start()
 
     wait_bytes(recv.at[COTX], cx)
     wait_bytes(recv.at[POOLX], px)
@@ -205,6 +229,11 @@
             part = part + mm(cx[i, r * half : (r + 1) * half], px[i], NN)
         n = others // parts
         cs[r * n : (r + 1) * n] = part.astype(jnp.bfloat16).reshape(n, erows, feats)
+
+    wait_bytes(recv.at[PROJ], pr.at[pl.ds(0, 2)])
+    far = ps[across_z].astype(jnp.float32) + pr[1].astype(jnp.float32)
+    pr[2] = far.astype(jnp.bfloat16)
+    remote(pr.at[2], pr.at[3], PROJZ, tp=across_z).start()
 
     def give(i, c):
         b = lax.rem(mehi + i, others)
@@ -238,19 +267,19 @@
         pair = jnp.concatenate([load_block(vt, lo), load_block(vt, hi)], axis=1)
         token_grad[lo * BLK : (hi + 1) * BLK] = mm(pair, w, NN).T.astype(jnp.bfloat16)
 
-    wait_bytes(recv.at[PROJ], pr)
-    proj = pr[0].astype(jnp.float32)
-    for i in range(1, ntp):
-        proj = proj + pr[i].astype(jnp.float32)
-    projected[...] = proj.astype(jnp.bfloat16)
+    wait_bytes(recv.at[PROJZ], pr.at[3])
+    near = ps[mytp].astype(jnp.float32) + pr[0].astype(jnp.float32)
+    projected[...] = (near + pr[3].astype(jnp.float32)).astype(jnp.bfloat16)
 
     wait_bytes(recv.at[GRAD], cr)
     proj_grad[...] = jnp.sum(cr[...].astype(jnp.float32), axis=0) * (1.0 / math.sqrt(npool * nt))
 
     for kind, ref in ((F_IN, yt), (B_IN, ut), (F_OUT, xr), (B_OUT, vt)):
         wait_bytes(send.at[kind], ref.at[pl.ds(0, nt - 1)])
-    wait_bytes(send.at[COT], cf.at[pl.ds(0, ntp - 1)])
-    wait_bytes(send.at[PROJ], pr.at[pl.ds(0, ntp - 1)])
+    wait_bytes(send.at[COT], cf.at[pl.ds(0, 2)])
+    wait_bytes(send.at[COTZ], cf.at[0])
+    wait_bytes(send.at[PROJ], pr.at[pl.ds(0, 2)])
+    wait_bytes(send.at[PROJZ], pr.at[0])
     wait_bytes(send.at[COTX], cx.at[pl.ds(0, NX - 1)])
     wait_bytes(send.at[POOLX], px.at[pl.ds(0, NX - 1)])
     mine = lax.div(me, others) == mex
@@ -264,7 +293,7 @@
         wait_bytes(send.at[GRAD], cr)
 
 
-def shards(nt, ntp, tokens, mixw, pw, pool_map, cot):
+def shards(nt, ntp, ny, tokens, mixw, pw, pool_map, cot):
     rows, feats = tokens.shape
     blocks = rows // BLK
     frows = feats * blocks // nt
@@ -275,7 +304,7 @@
     tiles = pltpu.VMEM((nt, frows, BLK), bf)
     vmem = pl.BlockSpec(memory_space=pltpu.VMEM)
     return pl.pallas_call(
-        functools.partial(kernel, nt, ntp),
+        functools.partial(kernel, nt, ntp, ny),
         out_shape=(
             jax.ShapeDtypeStruct((npool, equart), bf),
             jax.ShapeDtypeStruct((rows, feats), bf),
@@ -294,17 +323,18 @@
             pltpu.VMEM((ntp, npool, equart), bf),
             pltpu.VMEM((others, erows, feats), bf),
             pltpu.VMEM((others, erows, feats), bf),
-            pltpu.SemaphoreType.DMA((9,)),
-            pltpu.SemaphoreType.DMA((9,)),
+            pltpu.SemaphoreType.DMA((11,)),
+            pltpu.SemaphoreType.DMA((11,)),
+            pltpu.SemaphoreType.REGULAR((ny,)),
         ],
-        compiler_params=pltpu.CompilerParams(collective_id=0, has_side_effects=True),
+        compiler_params=pltpu.CompilerParams(collective_id=0, has_side_effects=True, vmem_limit_bytes=14 << 20),
     )(tokens, mixw, pw, pool_map.reshape(blocks, BLK), cot)
 
 
 def solution(mesh):
     nt, ntp = mesh.shape["tok"], mesh.shape["tp"]
     return jax.shard_map(
-        functools.partial(shards, nt, ntp),
+        functools.partial(shards, nt, ntp, nt // 16),
         mesh=mesh,
         in_specs=(P("tok", "tp"), P(), P("tp", None), P("tok"), P("tok", "tp")),
         out_specs=(P("tok", "tp"), P("tok", "tp"), P("tok", "tp")),

time: 115 us -> 111 us (0.965)
  the two profiles are of different devices: /device:TPU:1 before, /device:TPU:49 now
where the time goes in v2:
time: 111 us; the launch traced here: 110 us
  Pallas kernels  102 us (92%)
  local copies, waits for them, and re-layouts  7.22 us (7%)
    pallas_call x1, Pallas kernels, shards(): pl.pallas_call(functools.partial(kernel, nt, ntp, ny), out_shape=(jax.Sha...  102 us
    unnamed x13, local copies, waits for them, and re-layouts  7.22 us

profile of v2, /device:TPU:49, one launch (start us, length us, event | category | flops | bytes accessed | tf_op | source)
XLA Modules:
  0.0 110.3 jit_solution(2186908956214650576)
XLA Ops:
  0.6 0.0 copy-start
  0.6 1.3 %copy-done = bf16[10,2,2,128,128]{4,3,2,1,0:T(8,128)(2,1)S(1)} copy-done((bf16[10,2,2,128,128]{4,3,2,1,0:T(8,128)(2,1)S(1)}, bf16[10,2,2,128,128]{4,3,2,1,0:T(8,128)(2,1)}, u32[]{:S(2)}) %copy-start) | copy-done | bytes 1310744
  1.9 0.0 copy-start.1
  2.0 1.2 %copy-done.1 = bf16[256,2048]{1,0:T(8,128)(2,1)S(1)} copy-done((bf16[256,2048]{1,0:T(8,128)(2,1)S(1)}, bf16[256,2048]{1,0:T(8,128)(2,1)}, u32[]{:S(2)}) %copy-start.1) | copy-done | bytes 1048600
  3.2 0.0 copy-start.2
  3.2 1.0 copy-done.2
  4.2 0.0 copy-start.3
  4.2 0.9 copy-done.3
  5.1 0.0 copy-start.4
  5.1 0.7 copy-done.4
  5.8 102.4 %shard_map.76 = (bf16[128,512]{1,0:T(8,128)(2,1)S(1)}, bf16[1024,256]{1,0:T(8,128)(2,1)S(1)}, f32[16,256]{1,0:T(8,128)S(1)}) custom-call(bf16[1024,256]{1,0:T(8,128)(2,1)S(1)} %copy-done.2, bf16[10,2,2,128,128]{4,3,2,1,0:T(8,128)(2,1)S(1)} %copy-done, bf16[256,2048]{1,0:T(8,128)(2,1)S(1)} %copy-done.1, s32[8,128]{1,0:T(8,128)S(1)} %bitcast.1, ...), custom_call_target="tpu_custom_call" | custom-call | tf_op jit(solution)/shard_map/pallas_call | solution.py:306
  108.2 0.7 copy.11
  108.9 0.8 copy.12
  109.7 0.6 copy.13
Async XLA Ops:
  0.6 1.3 %copy-start = (bf16[10,2,2,128,128]{4,3,2,1,0:T(8,128)(2,1)S(1)}, bf16[10,2,2,128,128]{4,3,2,1,0:T(8,128)(2,1)}, u32[]{:S(2)}) copy-start(bf16[10,2,2,128,128]{4,3,2,1,0:T(8,128)(2,1)} %mixw.1) | copy-start | bytes 3932164
  1.9 1.2 %copy-start.1 = (bf16[256,2048]{1,0:T(8,128)(2,1)S(1)}, bf16[256,2048]{1,0:T(8,128)(2,1)}, u32[]{:S(2)}) copy-start(bf16[256,2048]{1,0:T(8,128)(2,1)} %pw.1) | copy-start | bytes 3145732
  3.2 1.0 copy-start.2
  4.2 0.9 copy-start.3
  5.1 0.7 copy-start.4

commit v3 on v2

--- a/solution.py
+++ b/solution.py
@@ -31,19 +31,31 @@
 
 
 def kernel(
-    nt, ntp, ny, tokens, mixw, pw, pmap, cot, projected, token_grad, proj_grad,
-    xs, yt, xr, gs, ut, vt, onehot, cf, cx, pool, px, ps, pr, cs, cr, send, recv, ready,
+    nt, ntp, ny, tokens_h, mixw_h, pw_h, pmap_h, cot_h, projected, token_grad, proj_grad,
+    tokens, mixw, pw, pmap, cot, load, xs, yt, xr, gs, ut, vt, onehot, cf, cx, pool, px, ps, pr, cs, cr, send, recv, ready,
 ):
     me = lax.axis_index("tok")
     mytp = lax.axis_index("tp")
-    feats = tokens.shape[1]
-    blocks = tokens.shape[0] // BLK
+    rows, feats = tokens.shape
+    blocks = rows // BLK
     groups = nt // blocks
     frows = feats // groups
     npool = cot.shape[0]
     equart = cot.shape[1]
     others = nt // NX
+    erows = proj_grad.shape[0]
     mex, mehi = lax.rem(me, NX), lax.div(me, NX)
+
+    loads = [
+        pltpu.make_async_copy(cot_h, cot, load.at[0]),
+        pltpu.make_async_copy(tokens_h, tokens, load.at[1]),
+        pltpu.make_async_copy(mixw_h.at[0:3], mixw.at[0:3], load.at[2]),
+        pltpu.make_async_copy(pmap_h, pmap, load.at[3]),
+        pltpu.make_async_copy(pw_h, pw, load.at[4]),
+        pltpu.make_async_copy(mixw_h.at[3:], mixw.at[3:], load.at[5]),
+    ]
+    for one in loads:
+        one.start()
 
     barrier = pltpu.get_barrier_semaphore()
     plane = nt // ny
@@ -64,7 +76,7 @@
     for i in range(1, ntp):
         pl.semaphore_signal(barrier, inc=1, device_id={"tp": lax.rem(mytp + i, ntp)}, device_id_type=MESH)
 
-    def exchange(kind, src, dst):
+    def exchange(kind, src, dst, first=0, last=nt):
         def one(i, c):
             d = lax.rem(me + i, nt)
             pltpu.make_async_remote_copy(
@@ -73,8 +85,9 @@
             ).start()
             return c
 
-        pltpu.make_async_copy(src.at[me], dst.at[me], recv.at[kind]).start()
-        lax.fori_loop(1, nt, one, 0)
+        if first == 0:
+            pltpu.make_async_copy(src.at[me], dst.at[me], recv.at[kind]).start()
+        lax.fori_loop(max(first, 1), last, one, 0)
 
     def remote(src, dst, kind, **to):
         return pltpu.make_async_remote_copy(
@@ -93,8 +106,11 @@
     def local_pairs(bit):
         return [(j, j | (1 << bit)) for j in range(blocks) if not j & (1 << bit)]
 
-    cf[mytp] = cot[...].astype(jnp.float32).T.astype(jnp.bfloat16)
-
+    loads[0].wait()
+    cf[mytp] = cot[...].astype(jnp.float32).T.astype(jnp.bfloat16).reshape(cf.shape[1:])
+
+    loads[1].wait()
+    loads[2].wait()
     w = section_matrix(mixw, 0)
     for lo, hi in local_pairs(0):
         out = mm(w, tokens[lo * BLK : (hi + 1) * BLK], NN).T.astype(jnp.bfloat16)
@@ -134,6 +150,7 @@
 
         lax.fori_loop(1 if k == 0 else 0, plane, to_plane, 0)
 
+    loads[3].wait()
     pid = lax.broadcasted_iota(jnp.int32, (npool, BLK), 0) + me * npool
     for j in range(blocks):
         hit = pid == jnp.broadcast_to(pmap[j : j + 1, :], (npool, BLK))
@@ -145,9 +162,10 @@
     wait_bytes(recv.at[COTZ], cf.at[0])
     remote(cf.at[across_z], cf.at[across_z], COT, tp=mate).start()
     wait_bytes(recv.at[COT], cf.at[pl.ds(0, 2)])
-    dp = mm(pw[:, 0:equart], cf[0], NN)
+    loads[4].wait()
+    dp = mm(pw[:, 0:equart], cf[0].reshape(equart, npool), NN)
     for i in range(1, ntp):
-        dp = dp + mm(pw[:, i * equart : (i + 1) * equart], cf[i], NN)
+        dp = dp + mm(pw[:, i * equart : (i + 1) * equart], cf[i].reshape(equart, npool), NN)
     dp = (dp / counts_row).astype(jnp.bfloat16)
     for j in range(blocks):
         store_block(gs, j, mm(dp, onehot[:, j * BLK : (j + 1) * BLK], NN).astype(jnp.bfloat16))
@@ -156,10 +174,10 @@
     for i in range(NX):
         dx = lax.rem(mex + i, NX)
         if i == 0:
-            pltpu.make_async_copy(cf.at[dx], cx.at[mex], recv.at[COTX]).start()
+            pltpu.make_async_copy(cf.at[:, :, dx], cx.at[mex], recv.at[COTX]).start()
         else:
             pltpu.make_async_remote_copy(
-                src_ref=cf.at[dx], dst_ref=cx.at[mex], send_sem=send.at[COTX], recv_sem=recv.at[COTX],
+                src_ref=cf.at[:, :, dx], dst_ref=cx.at[mex], send_sem=send.at[COTX], recv_sem=recv.at[COTX],
                 device_id={"tok": mehi * NX + dx}, device_id_type=MESH,
             ).start()
 
@@ -189,6 +207,7 @@
                 ref[base : base + 2 * run] = jnp.concatenate([a, b], axis=1).reshape(2 * run, frows, BLK)
 
     bits = nt.bit_length() - 1
+    loads[5].wait()
     wait_bytes(recv.at[F_IN], yt)
     for bit in range(bits):
         across(yt, bit, 3 + bit, NT)
@@ -197,7 +216,7 @@
     wait_bytes(recv.at[B_IN], ut)
     for bit in reversed(range(bits)):
         across(ut, bit, 3 + bit, NN)
-    exchange(B_OUT, ut, vt)
+    exchange(B_OUT, ut, vt, 0, nt // 2)
 
     wait_bytes(recv.at[F_OUT], xr)
     total = mm(onehot[:, 0:BLK], load_block(xr, 0), NT)
@@ -217,42 +236,29 @@
         ps[i] = mm(pool[...], pw[:, i * equart : (i + 1) * equart], NN).astype(jnp.bfloat16)
     remote(ps.at[mate], pr.at[0], PROJ, tp=mate).start()
     remote(ps.at[diagonal], pr.at[1], PROJ, tp=mate).start()
+    exchange(B_OUT, ut, vt, nt // 2, nt)
 
     wait_bytes(recv.at[COTX], cx)
     wait_bytes(recv.at[POOLX], px)
-    erows = equart // others
-    parts = min(4, others)
-    half = equart // parts
-    for r in range(parts):
-        part = mm(cx[0, r * half : (r + 1) * half], px[0], NN)
+    for q in range(ntp):
+        n = others // ntp
+        part = mm(cx[0, q].reshape(n * erows, npool), px[0], NN)
         for i in range(1, NX):
-            part = part + mm(cx[i, r * half : (r + 1) * half], px[i], NN)
-        n = others // parts
-        cs[r * n : (r + 1) * n] = part.astype(jnp.bfloat16).reshape(n, erows, feats)
+            part = part + mm(cx[i, q].reshape(n * erows, npool), px[i], NN)
+        cs[q * n : (q + 1) * n] = part.astype(jnp.bfloat16).reshape(n, erows, feats)
+
+    def give(i, c):
+        b = lax.rem(mehi + i, others)
+        remote(cs.at[b], cr.at[mehi], GRAD, tok=b * NX + mex).start()
+        return c
+
+    pltpu.make_async_copy(cs.at[mehi], cr.at[mehi], recv.at[GRAD]).start()
+    lax.fori_loop(1, others, give, 0)
 
     wait_bytes(recv.at[PROJ], pr.at[pl.ds(0, 2)])
     far = ps[across_z].astype(jnp.float32) + pr[1].astype(jnp.float32)
     pr[2] = far.astype(jnp.bfloat16)
     remote(pr.at[2], pr.at[3], PROJZ, tp=across_z).start()
-
-    def give(i, c):
-        b = lax.rem(mehi + i, others)
-        d = mex * others + b
-
-        @pl.when(d == me)
-        def _():
-            pltpu.make_async_copy(cs.at[b], cr.at[mehi], recv.at[GRAD]).start()
-
-        @pl.when(d != me)
-        def _():
-            pltpu.make_async_remote_copy(
-                src_ref=cs.at[b], dst_ref=cr.at[mehi], send_sem=send.at[GRAD], recv_sem=recv.at[GRAD],
-                device_id={"tok": d}, device_id_type=MESH,
-            ).start()
-
-        return c
-
-    lax.fori_loop(0, others, give, 0)
 
     wait_bytes(recv.at[B_OUT], vt)
     for bit in (2, 1):
@@ -282,15 +288,7 @@
     wait_bytes(send.at[PROJZ], pr.at[0])
     wait_bytes(send.at[COTX], cx.at[pl.ds(0, NX - 1)])
     wait_bytes(send.at[POOLX], px.at[pl.ds(0, NX - 1)])
-    mine = lax.div(me, others) == mex
-
-    @pl.when(mine)
-    def _():
-        wait_bytes(send.at[GRAD], cr.at[pl.ds(0, others - 1)])
-
-    @pl.when(jnp.logical_not(mine))
-    def _():
-        wait_bytes(send.at[GRAD], cr)
+    wait_bytes(send.at[GRAD], cr.at[pl.ds(0, others - 1)])
 
 
 def shards(nt, ntp, ny, tokens, mixw, pw, pool_map, cot):
@@ -300,6 +298,7 @@
     npool, equart = cot.shape
     others = nt // NX
     erows = equart // others
+    share = equart // (NX * erows)
     bf = jnp.bfloat16
     tiles = pltpu.VMEM((nt, frows, BLK), bf)
     vmem = pl.BlockSpec(memory_space=pltpu.VMEM)
@@ -310,13 +309,19 @@
             jax.ShapeDtypeStruct((rows, feats), bf),
             jax.ShapeDtypeStruct((erows, feats), jnp.float32),
         ),
-        in_specs=[vmem] * 5,
+        in_specs=[pl.BlockSpec(memory_space=pltpu.HBM)] * 5,
         out_specs=(vmem,) * 3,
         scratch_shapes=[
+            pltpu.VMEM((rows, feats), bf),
+            pltpu.VMEM(mixw.shape, bf),
+            pltpu.VMEM(pw.shape, bf),
+            pltpu.VMEM((blocks, BLK), jnp.int32),
+            pltpu.VMEM((npool, equart), bf),
+            pltpu.SemaphoreType.DMA((6,)),
             tiles, tiles, tiles, tiles, tiles, tiles,
             pltpu.VMEM((npool, rows), bf),
-            pltpu.VMEM((ntp, equart, npool), bf),
-            pltpu.VMEM((NX, equart, npool), bf),
+            pltpu.VMEM((ntp, share, NX, erows, npool), bf),
+            pltpu.VMEM((NX, ntp, share, erows, npool), bf),
             pltpu.VMEM((npool, feats), bf),
             pltpu.VMEM((NX, npool, feats), bf),
             pltpu.VMEM((ntp, npool, equart), bf),
@@ -327,7 +332,7 @@
             pltpu.SemaphoreType.DMA((11,)),
             pltpu.SemaphoreType.REGULAR((ny,)),
         ],
-        compiler_params=pltpu.CompilerParams(collective_id=0, has_side_effects=True, vmem_limit_bytes=14 << 20),
+        compiler_params=pltpu.CompilerParams(collective_id=0, has_side_effects=True, vmem_limit_bytes=18 << 20),
     )(tokens, mixw, pw, pool_map.reshape(blocks, BLK), cot)
 
 

time: 111 us -> 90.9 us (0.82)
  the two profiles are of different devices: /device:TPU:49 before, /device:TPU:1 now
where the time goes in v3:
time: 90.9 us; the launch traced here: 90.6 us
  Pallas kernels  82.7 us (91%)
  local copies, waits for them, and re-layouts  7.22 us (8%)
    pallas_call x1, Pallas kernels, shards(): pl.pallas_call(functools.partial(kernel, nt, ntp, ny), out_shape=(jax.Sha...  82.7 us
    unnamed x13, local copies, waits for them, and re-layouts  7.22 us

profile of v3, /device:TPU:1, one launch (start us, length us, event | category | flops | bytes accessed | tf_op | source)
XLA Modules:
  0.0 90.6 jit_solution(3466894616917420653)
XLA Ops:
  0.6 0.0 copy-start
  0.6 1.3 %copy-done = bf16[10,2,2,128,128]{4,3,2,1,0:T(8,128)(2,1)S(1)} copy-done((bf16[10,2,2,128,128]{4,3,2,1,0:T(8,128)(2,1)S(1)}, bf16[10,2,2,128,128]{4,3,2,1,0:T(8,128)(2,1)}, u32[]{:S(2)}) %copy-start) | copy-done | bytes 1310744
  1.9 0.0 copy-start.1
  2.0 1.2 %copy-done.1 = bf16[256,2048]{1,0:T(8,128)(2,1)S(1)} copy-done((bf16[256,2048]{1,0:T(8,128)(2,1)S(1)}, bf16[256,2048]{1,0:T(8,128)(2,1)}, u32[]{:S(2)}) %copy-start.1) | copy-done | bytes 1048600
  3.2 0.0 copy-start.2
  3.2 1.0 %copy-done.2 = bf16[1024,256]{1,0:T(8,128)(2,1)S(1)} copy-done((bf16[1024,256]{1,0:T(8,128)(2,1)S(1)}, bf16[1024,256]{1,0:T(8,128)(2,1)}, u32[]{:S(2)}) %copy-start.2) | copy-done | bytes 524312
  4.2 0.0 copy-start.3
  4.2 0.9 copy-done.3
  5.1 0.0 copy-start.4
  5.1 0.7 copy-done.4
  5.8 82.7 %shard_map.76 = (bf16[128,512]{1,0:T(8,128)(2,1)S(1)}, bf16[1024,256]{1,0:T(8,128)(2,1)S(1)}, f32[16,256]{1,0:T(8,128)S(1)}) custom-call(bf16[1024,256]{1,0:T(8,128)(2,1)S(1)} %copy-done.2, bf16[10,2,2,128,128]{4,3,2,1,0:T(8,128)(2,1)S(1)} %copy-done, bf16[256,2048]{1,0:T(8,128)(2,1)S(1)} %copy-done.1, s32[8,128]{1,0:T(8,128)S(1)} %bitcast.1, ...), custom_call_target="tpu_custom_call" | custom-call | tf_op jit(solution)/shard_map/pallas_call | solution.py:305
  88.6 0.7 copy.11
  89.2 0.8 copy.12
  90.0 0.6 copy.13
Async XLA Ops:
  0.6 1.3 %copy-start = (bf16[10,2,2,128,128]{4,3,2,1,0:T(8,128)(2,1)S(1)}, bf16[10,2,2,128,128]{4,3,2,1,0:T(8,128)(2,1)}, u32[]{:S(2)}) copy-start(bf16[10,2,2,128,128]{4,3,2,1,0:T(8,128)(2,1)} %mixw_h.1) | copy-start | bytes 3932164
  1.9 1.2 %copy-start.1 = (bf16[256,2048]{1,0:T(8,128)(2,1)S(1)}, bf16[256,2048]{1,0:T(8,128)(2,1)}, u32[]{:S(2)}) copy-start(bf16[256,2048]{1,0:T(8,128)(2,1)} %pw_h.1) | copy-start | bytes 3145732
  3.2 1.0 %copy-start.2 = (bf16[1024,256]{1,0:T(8,128)(2,1)S(1)}, bf16[1024,256]{1,0:T(8,128)(2,1)}, u32[]{:S(2)}) copy-start(bf16[1024,256]{1,0:T(8,128)(2,1)} %tokens_h.1) | copy-start | bytes 1572868
  4.2 0.9 copy-start.3
  5.1 0.7 copy-start.4

commit v4 on v3

--- a/solution.py
+++ b/solution.py
@@ -13,7 +13,7 @@
 NX = 4
 NN = (((1,), (0,)), ((), ()))
 NT = (((1,), (1,)), ((), ()))
-F_IN, F_OUT, B_IN, B_OUT, COT, COTX, POOLX, PROJ, GRAD, COTZ, PROJZ = range(11)
+F_IN, F_OUT, B_OUT, COT, COTX, POOLX, PROJ, GRAD, COTZ, PROJZ, DY, DZ, DX, MY, MZ, MX = range(16)
 
 
 def mm(a, b, dims):
@@ -32,7 +32,7 @@
 
 def kernel(
     nt, ntp, ny, tokens_h, mixw_h, pw_h, pmap_h, cot_h, projected, token_grad, proj_grad,
-    tokens, mixw, pw, pmap, cot, load, xs, yt, xr, gs, ut, vt, onehot, cf, cx, pool, px, ps, pr, cs, cr, send, recv, ready,
+    tokens, mixw, pw, pmap, cot, load, xs, yt, xr, ut, vt, d0, d1, d2, d3, m1, m2, m3, onehot, cf, cx, pool, px, ps, pr, cs, cr, send, recv, ready,
 ):
     me = lax.axis_index("tok")
     mytp = lax.axis_index("tp")
@@ -45,6 +45,8 @@
     others = nt // NX
     erows = proj_grad.shape[0]
     mex, mehi = lax.rem(me, NX), lax.div(me, NX)
+    nz = nt // (ny * NX)
+    myz = lax.rem(mehi, nz)
 
     loads = [
         pltpu.make_async_copy(cot_h, cot, load.at[0]),
@@ -153,7 +155,7 @@
     loads[3].wait()
     pid = lax.broadcasted_iota(jnp.int32, (npool, BLK), 0) + me * npool
     for j in range(blocks):
-        hit = pid == jnp.broadcast_to(pmap[j : j + 1, :], (npool, BLK))
+        hit = pid == jnp.broadcast_to(pmap[j], (npool, BLK))
         onehot[:, j * BLK : (j + 1) * BLK] = jnp.where(hit, 1.0, 0.0).astype(jnp.bfloat16)
     ones = jnp.ones((8, blocks * BLK), jnp.bfloat16)
     counts_row = mm(ones, onehot[...], NT)[0:1]
@@ -167,9 +169,20 @@
     for i in range(1, ntp):
         dp = dp + mm(pw[:, i * equart : (i + 1) * equart], cf[i].reshape(equart, npool), NN)
     dp = (dp / counts_row).astype(jnp.bfloat16)
-    for j in range(blocks):
-        store_block(gs, j, mm(dp, onehot[:, j * BLK : (j + 1) * BLK], NN).astype(jnp.bfloat16))
-    exchange(B_IN, gs, ut)
+    d0[...] = dp.reshape(groups, frows, npool)
+
+    def along(size, mine, target, pairs):
+        for src, dst, kind in pairs:
+            pltpu.make_async_copy(src(mine), dst, recv.at[kind]).start()
+        for i in range(1, size):
+            to = lax.rem(mine + i, size)
+            for src, dst, kind in pairs:
+                remote(src(to), dst, kind, tok=target(to)).start()
+
+    along(
+        ny, myy, lambda y: y * plane + myp,
+        [(lambda y: d0.at[pl.ds(2 * y, 2)], d1.at[myy], DY), (lambda y: pmap, m1.at[myy], MY)],
+    )
 
     for i in range(NX):
         dx = lax.rem(mex + i, NX)
@@ -207,13 +220,36 @@
                 ref[base : base + 2 * run] = jnp.concatenate([a, b], axis=1).reshape(2 * run, frows, BLK)
 
     bits = nt.bit_length() - 1
+    wait_bytes(recv.at[DY], d1)
+    wait_bytes(recv.at[MY], m1)
+    along(
+        nz, myz, lambda z: myy * plane + z * NX + mex,
+        [
+            (lambda z: d1.at[:, lax.div(z, 2)], d2.at[myz], DZ),
+            (lambda z: m1.at[:, pl.ds(lax.rem(z, 2) * NX, NX)], m2.at[myz], MZ),
+        ],
+    )
+
     loads[5].wait()
     wait_bytes(recv.at[F_IN], yt)
     for bit in range(bits):
         across(yt, bit, 3 + bit, NT)
+
+    wait_bytes(recv.at[DZ], d2)
+    wait_bytes(recv.at[MZ], m2)
+    along(
+        NX, mex, lambda x: mehi * NX + x,
+        [(lambda x: d2, d3.at[mex], DX), (lambda x: m2.at[:, :, x], m3.at[mex], MX)],
+    )
     exchange(F_OUT, yt, xr)
 
-    wait_bytes(recv.at[B_IN], ut)
+    wait_bytes(recv.at[DX], d3)
+    wait_bytes(recv.at[MX], m3)
+    rank = lax.broadcasted_iota(jnp.int32, (npool, BLK), 0)
+    for t in range(nt):
+        at = (t % NX, t // NX % nz, t // NX // nz)
+        hit = rank == jnp.broadcast_to(m3[at] - t * npool, (npool, BLK))
+        ut[t] = mm(d3[at], jnp.where(hit, 1.0, 0.0).astype(jnp.bfloat16), NN).astype(jnp.bfloat16)
     for bit in reversed(range(bits)):
         across(ut, bit, 3 + bit, NN)
     exchange(B_OUT, ut, vt, 0, nt // 2)
@@ -280,8 +316,10 @@
     wait_bytes(recv.at[GRAD], cr)
     proj_grad[...] = jnp.sum(cr[...].astype(jnp.float32), axis=0) * (1.0 / math.sqrt(npool * nt))
 
-    for kind, ref in ((F_IN, yt), (B_IN, ut), (F_OUT, xr), (B_OUT, vt)):
+    for kind, ref in ((F_IN, yt), (F_OUT, xr), (B_OUT, vt)):
         wait_bytes(send.at[kind], ref.at[pl.ds(0, nt - 1)])
+    for kind, ref in ((DY, d1), (DZ, d2), (DX, d3), (MY, m1), (MZ, m2), (MX, m3)):
+        wait_bytes(send.at[kind], ref.at[pl.ds(0, ref.shape[0] - 1)])
     wait_bytes(send.at[COT], cf.at[pl.ds(0, 2)])
     wait_bytes(send.at[COTZ], cf.at[0])
     wait_bytes(send.at[PROJ], pr.at[pl.ds(0, 2)])
@@ -294,7 +332,9 @@
 def shards(nt, ntp, ny, tokens, mixw, pw, pool_map, cot):
     rows, feats = tokens.shape
     blocks = rows // BLK
-    frows = feats * blocks // nt
+    groups = nt // blocks
+    frows = feats // groups
+    nz = nt // (ny * NX)
     npool, equart = cot.shape
     others = nt // NX
     erows = equart // others
@@ -315,10 +355,17 @@
             pltpu.VMEM((rows, feats), bf),
             pltpu.VMEM(mixw.shape, bf),
             pltpu.VMEM(pw.shape, bf),
-            pltpu.VMEM((blocks, BLK), jnp.int32),
+            pltpu.VMEM((blocks, 1, BLK), jnp.int32),
             pltpu.VMEM((npool, equart), bf),
             pltpu.SemaphoreType.DMA((6,)),
-            tiles, tiles, tiles, tiles, tiles, tiles,
+            tiles, tiles, tiles, tiles, tiles,
+            pltpu.VMEM((groups, frows, npool), bf),
+            pltpu.VMEM((ny, 2, frows, npool), bf),
+            pltpu.VMEM((nz, ny, frows, npool), bf),
+            pltpu.VMEM((NX, nz, ny, frows, npool), bf),
+            pltpu.VMEM((ny, blocks, 1, BLK), jnp.int32),
+            pltpu.VMEM((nz, ny, NX, 1, BLK), jnp.int32),
+            pltpu.VMEM((NX, nz, ny, 1, BLK), jnp.int32),
             pltpu.VMEM((npool, rows), bf),
             pltpu.VMEM((ntp, share, NX, erows, npool), bf),
             pltpu.VMEM((NX, ntp, share, erows, npool), bf),
@@ -328,12 +375,12 @@
             pltpu.VMEM((ntp, npool, equart), bf),
             pltpu.VMEM((others, erows, feats), bf),
             pltpu.VMEM((others, erows, feats), bf),
-            pltpu.SemaphoreType.DMA((11,)),
-            pltpu.SemaphoreType.DMA((11,)),
+            pltpu.SemaphoreType.DMA((16,)),
+            pltpu.SemaphoreType.DMA((16,)),
             pltpu.SemaphoreType.REGULAR((ny,)),
         ],
         compiler_params=pltpu.CompilerParams(collective_id=0, has_side_effects=True, vmem_limit_bytes=18 << 20),
-    )(tokens, mixw, pw, pool_map.reshape(blocks, BLK), cot)
+    )(*[pltpu.with_memory_space_constraint(a, pltpu.HBM) for a in (tokens, mixw, pw, pool_map.reshape(blocks, 1, BLK), cot)])
 
 
 def solution(mesh):

time: 90.9 us -> 86.3 us (0.949)
  local copies, waits for them, and re-layouts: 7.22 us -> 2.06 us
    unnamed x13 -> x3, local copies, waits for them, and re-layouts: 7.22 us -> 2.06 us
where the time goes in v4:
time: 86.3 us; the launch traced here: 86.2 us
  Pallas kernels  83.5 us (97%)
  local copies, waits for them, and re-layouts  2.06 us (2%)
    pallas_call x1, Pallas kernels, shards(): pl.pallas_call(functools.partial(kernel, nt, ntp, ny), out_shape=(jax.Sha...  83.5 us
    unnamed x3, local copies, waits for them, and re-layouts  2.06 us

profile of v4, /device:TPU:1, one launch (start us, length us, event | category | flops | bytes accessed | tf_op | source)
XLA Modules:
  0.0 86.2 jit_solution(3220417467765981118)
XLA Ops:
  0.6 83.5 %shard_map.76 = (bf16[128,512]{1,0:T(8,128)(2,1)S(1)}, bf16[1024,256]{1,0:T(8,128)(2,1)S(1)}, f32[16,256]{1,0:T(8,128)S(1)}) custom-call(bf16[1024,256]{1,0:T(8,128)(2,1)} %tokens_h.1, bf16[10,2,2,128,128]{4,3,2,1,0:T(8,128)(2,1)} %mixw_h.1, bf16[256,2048]{1,0:T(8,128)(2,1)} %pw_h.1, s32[8,1,128]{2,1,0:T(1,128)} %bitcast.1, bf16[128,512]{1,0:T(8,128)(2,1)} %cot_h.1), custom_call_target="tpu_custom_call" | custom-call | tf_op jit(solution)/shard_map/pallas_call | solution.py:345
  84.1 0.7 copy.11
  84.8 0.8 copy.12
  85.6 0.6 copy.13

commit v5 on v4

--- a/solution.py
+++ b/solution.py
@@ -13,7 +13,8 @@
 NX = 4
 NN = (((1,), (0,)), ((), ()))
 NT = (((1,), (1,)), ((), ()))
-F_IN, F_OUT, B_OUT, COT, COTX, POOLX, PROJ, GRAD, COTZ, PROJZ, DY, DZ, DX, MY, MZ, MX = range(16)
+F_IN, F_OUT, B_OUT, COT, COTX, POOLX, PROJ, GRAD, COTZ, PROJZ, DY, DZ, MY, MZ = range(14)
+DX, MX = 14, 18
 
 
 def mm(a, b, dims):
@@ -139,18 +140,22 @@
     remote(cf.at[mytp], cf.at[mytp], COT, tp=mate).start()
 
     pltpu.make_async_copy(xs.at[me], yt.at[me], recv.at[F_IN]).start()
-    for k in range(ny):
-        step = (k + 1) // 2 if k % 2 else ny - k // 2
-        y = lax.rem(myy + step, ny)
-        if k > 0:
-            pl.semaphore_wait(ready.at[y], 1)
-
-        def to_plane(i, c, y=y):
-            d = y * plane + lax.rem(myp + i, plane)
-            remote(xs.at[d], yt.at[me], F_IN, tok=d).start()
-            return c
-
-        lax.fori_loop(1 if k == 0 else 0, plane, to_plane, 0)
+    order = [0] + sorted(range(1, ny), key=lambda step: -min(step, ny - step))
+
+    def send_planes(steps):
+        for step in steps:
+            y = lax.rem(myy + step, ny)
+            if step > 0:
+                pl.semaphore_wait(ready.at[y], 1)
+
+            def to_plane(i, c, y=y):
+                d = y * plane + lax.rem(myp + i, plane)
+                remote(xs.at[d], yt.at[me], F_IN, tok=d).start()
+                return c
+
+            lax.fori_loop(0 if step > 0 else 1, plane, to_plane, 0)
+
+    send_planes(order[: ny // 2])
 
     loads[3].wait()
     pid = lax.broadcasted_iota(jnp.int32, (npool, BLK), 0) + me * npool
@@ -184,15 +189,7 @@
         [(lambda y: d0.at[pl.ds(2 * y, 2)], d1.at[myy], DY), (lambda y: pmap, m1.at[myy], MY)],
     )
 
-    for i in range(NX):
-        dx = lax.rem(mex + i, NX)
-        if i == 0:
-            pltpu.make_async_copy(cf.at[:, :, dx], cx.at[mex], recv.at[COTX]).start()
-        else:
-            pltpu.make_async_remote_copy(
-                src_ref=cf.at[:, :, dx], dst_ref=cx.at[mex], send_sem=send.at[COTX], recv_sem=recv.at[COTX],
-                device_id={"tok": mehi * NX + dx}, device_id_type=MESH,
-            ).start()
+    send_planes(order[ny // 2 :])
 
     def across(ref, bit, s, dims):
         w = section_matrix(mixw, s)
@@ -237,19 +234,35 @@
 
     wait_bytes(recv.at[DZ], d2)
     wait_bytes(recv.at[MZ], m2)
-    along(
-        NX, mex, lambda x: mehi * NX + x,
-        [(lambda x: d2, d3.at[mex], DX), (lambda x: m2.at[:, :, x], m3.at[mex], MX)],
-    )
+    for i in range(1, NX):
+        x = lax.rem(mex + i, NX)
+        remote(d2, d3.at[mex], DX + i, tok=mehi * NX + x).start()
+        remote(m2.at[:, :, x], m3.at[mex], MX + i, tok=mehi * NX + x).start()
     exchange(F_OUT, yt, xr)
 
-    wait_bytes(recv.at[DX], d3)
-    wait_bytes(recv.at[MX], m3)
+    for i in range(NX):
+        dx = lax.rem(mex + i, NX)
+        if i == 0:
+            pltpu.make_async_copy(cf.at[:, :, dx], cx.at[mex], recv.at[COTX]).start()
+        else:
+            pltpu.make_async_remote_copy(
+                src_ref=cf.at[:, :, dx], dst_ref=cx.at[mex], send_sem=send.at[COTX], recv_sem=recv.at[COTX],
+                device_id={"tok": mehi * NX + dx}, device_id_type=MESH,
+            ).start()
+
     rank = lax.broadcasted_iota(jnp.int32, (npool, BLK), 0)
-    for t in range(nt):
-        at = (t % NX, t // NX % nz, t // NX // nz)
-        hit = rank == jnp.broadcast_to(m3[at] - t * npool, (npool, BLK))
-        ut[t] = mm(d3[at], jnp.where(hit, 1.0, 0.0).astype(jnp.bfloat16), NN).astype(jnp.bfloat16)
+    for i in range(NX):
+        x = lax.rem(mex - i + NX, NX)
+        if i > 0:
+            wait_bytes(recv.at[DX + i], d2)
+            wait_bytes(recv.at[MX + i], m3.at[0])
+        for z in range(nz):
+            for y in range(ny):
+                t = (y * nz + z) * NX + x
+                row = (m2[z, y, mex] if i == 0 else m3[x, z, y]) - t * npool
+                hit = rank == jnp.broadcast_to(row, (npool, BLK))
+                rows_in = d2[z, y] if i == 0 else d3[x, z, y]
+                ut[t] = mm(rows_in, jnp.where(hit, 1.0, 0.0).astype(jnp.bfloat16), NN).astype(jnp.bfloat16)
     for bit in reversed(range(bits)):
         across(ut, bit, 3 + bit, NN)
     exchange(B_OUT, ut, vt, 0, nt // 2)
@@ -318,7 +331,10 @@
 
     for kind, ref in ((F_IN, yt), (F_OUT, xr), (B_OUT, vt)):
         wait_bytes(send.at[kind], ref.at[pl.ds(0, nt - 1)])
-    for kind, ref in ((DY, d1), (DZ, d2), (DX, d3), (MY, m1), (MZ, m2), (MX, m3)):
+    for i in range(1, NX):
+        wait_bytes(send.at[DX + i], d2)
+        wait_bytes(send.at[MX + i], m3.at[0])
+    for kind, ref in ((DY, d1), (DZ, d2), (MY, m1), (MZ, m2)):
         wait_bytes(send.at[kind], ref.at[pl.ds(0, ref.shape[0] - 1)])
     wait_bytes(send.at[COT], cf.at[pl.ds(0, 2)])
     wait_bytes(send.at[COTZ], cf.at[0])
@@ -375,8 +391,8 @@
             pltpu.VMEM((ntp, npool, equart), bf),
             pltpu.VMEM((others, erows, feats), bf),
             pltpu.VMEM((others, erows, feats), bf),
-            pltpu.SemaphoreType.DMA((16,)),
-            pltpu.SemaphoreType.DMA((16,)),
+            pltpu.SemaphoreType.DMA((22,)),
+            pltpu.SemaphoreType.DMA((22,)),
             pltpu.SemaphoreType.REGULAR((ny,)),
         ],
         compiler_params=pltpu.CompilerParams(collective_id=0, has_side_effects=True, vmem_limit_bytes=18 << 20),

time: 86.3 us -> 84.1 us (0.975)
  Pallas kernels: 83.5 us -> 81.2 us
    pallas_call x1, Pallas kernels: 83.5 us -> 81.2 us  [shards(): pl.pallas_call(functools.partial(kernel, nt, ntp, ny), out_shape=(jax.Sha...]
where the time goes in v5:
time: 84.1 us; the launch traced here: 83.9 us
  Pallas kernels  81.2 us (97%)
  local copies, waits for them, and re-layouts  2.06 us (2%)
    pallas_call x1, Pallas kernels, shards(): pl.pallas_call(functools.partial(kernel, nt, ntp, ny), out_shape=(jax.Sha...  81.2 us
    unnamed x3, local copies, waits for them, and re-layouts  2.06 us

profile of v5, /device:TPU:1, one launch (start us, length us, event | category | flops | bytes accessed | tf_op | source)
XLA Modules:
  0.0 83.9 jit_solution(2510215991702921674)
XLA Ops:
  0.6 81.2 %shard_map.76 = (bf16[128,512]{1,0:T(8,128)(2,1)S(1)}, bf16[1024,256]{1,0:T(8,128)(2,1)S(1)}, f32[16,256]{1,0:T(8,128)S(1)}) custom-call(bf16[1024,256]{1,0:T(8,128)(2,1)} %tokens_h.1, bf16[10,2,2,128,128]{4,3,2,1,0:T(8,128)(2,1)} %mixw_h.1, bf16[256,2048]{1,0:T(8,128)(2,1)} %pw_h.1, s32[8,1,128]{2,1,0:T(1,128)} %bitcast.1, bf16[128,512]{1,0:T(8,128)(2,1)} %cot_h.1), custom_call_target="tpu_custom_call" | custom-call | tf_op jit(solution)/shard_map/pallas_call | solution.py:361
  81.9 0.7 copy.11
  82.5 0.8 copy.12
  83.3 0.6 copy.13

commit v6 on v5

--- a/solution.py
+++ b/solution.py
@@ -190,6 +190,16 @@
     )
 
     send_planes(order[ny // 2 :])
+
+    for i in range(NX):
+        dx = lax.rem(mex + i, NX)
+        if i == 0:
+            pltpu.make_async_copy(cf.at[:, :, dx], cx.at[mex], recv.at[COTX]).start()
+        else:
+            pltpu.make_async_remote_copy(
+                src_ref=cf.at[:, :, dx], dst_ref=cx.at[mex], send_sem=send.at[COTX], recv_sem=recv.at[COTX],
+                device_id={"tok": mehi * NX + dx}, device_id_type=MESH,
+            ).start()
 
     def across(ref, bit, s, dims):
         w = section_matrix(mixw, s)
@@ -239,16 +249,6 @@
         remote(d2, d3.at[mex], DX + i, tok=mehi * NX + x).start()
         remote(m2.at[:, :, x], m3.at[mex], MX + i, tok=mehi * NX + x).start()
     exchange(F_OUT, yt, xr)
-
-    for i in range(NX):
-        dx = lax.rem(mex + i, NX)
-        if i == 0:
-            pltpu.make_async_copy(cf.at[:, :, dx], cx.at[mex], recv.at[COTX]).start()
-        else:
-            pltpu.make_async_remote_copy(
-                src_ref=cf.at[:, :, dx], dst_ref=cx.at[mex], send_sem=send.at[COTX], recv_sem=recv.at[COTX],
-                device_id={"tok": mehi * NX + dx}, device_id_type=MESH,
-            ).start()
 
     rank = lax.broadcasted_iota(jnp.int32, (npool, BLK), 0)
     for i in range(NX):
@@ -287,6 +287,11 @@
     remote(ps.at[diagonal], pr.at[1], PROJ, tp=mate).start()
     exchange(B_OUT, ut, vt, nt // 2, nt)
 
+    wait_bytes(recv.at[PROJ], pr.at[pl.ds(0, 2)])
+    far = ps[across_z].astype(jnp.float32) + pr[1].astype(jnp.float32)
+    pr[2] = far.astype(jnp.bfloat16)
+    remote(pr.at[2], pr.at[3], PROJZ, tp=across_z).start()
+
     wait_bytes(recv.at[COTX], cx)
     wait_bytes(recv.at[POOLX], px)
     for q in range(ntp):
@@ -303,11 +308,6 @@
 
     pltpu.make_async_copy(cs.at[mehi], cr.at[mehi], recv.at[GRAD]).start()
     lax.fori_loop(1, others, give, 0)
-
-    wait_bytes(recv.at[PROJ], pr.at[pl.ds(0, 2)])
-    far = ps[across_z].astype(jnp.float32) + pr[1].astype(jnp.float32)
-    pr[2] = far.astype(jnp.bfloat16)
-    remote(pr.at[2], pr.at[3], PROJZ, tp=across_z).start()
 
     wait_bytes(recv.at[B_OUT], vt)
     for bit in (2, 1):

time: 84.1 us -> 82.6 us (0.982)
  Pallas kernels: 81.2 us -> 79.8 us
    pallas_call x1, Pallas kernels: 81.2 us -> 79.8 us  [shards(): pl.pallas_call(functools.partial(kernel, nt, ntp, ny), out_shape=(jax.Sha...]
where the time goes in v6:
time: 82.6 us; the launch traced here: 82.5 us
  Pallas kernels  79.8 us (97%)
  local copies, waits for them, and re-layouts  2.06 us (2%)
    pallas_call x1, Pallas kernels, shards(): pl.pallas_call(functools.partial(kernel, nt, ntp, ny), out_shape=(jax.Sha...  79.8 us
    unnamed x3, local copies, waits for them, and re-layouts  2.06 us

profile of v6, /device:TPU:1, one launch (start us, length us, event | category | flops | bytes accessed | tf_op | source)
XLA Modules:
  0.0 82.5 jit_solution(4219130000541681098)
XLA Ops:
  0.6 79.8 %shard_map.76 = (bf16[128,512]{1,0:T(8,128)(2,1)S(1)}, bf16[1024,256]{1,0:T(8,128)(2,1)S(1)}, f32[16,256]{1,0:T(8,128)S(1)}) custom-call(bf16[1024,256]{1,0:T(8,128)(2,1)} %tokens_h.1, bf16[10,2,2,128,128]{4,3,2,1,0:T(8,128)(2,1)} %mixw_h.1, bf16[256,2048]{1,0:T(8,128)(2,1)} %pw_h.1, s32[8,1,128]{2,1,0:T(1,128)} %bitcast.1, bf16[128,512]{1,0:T(8,128)(2,1)} %cot_h.1), custom_call_target="tpu_custom_call" | custom-call | tf_op jit(solution)/shard_map/pallas_call | solution.py:361
  80.4 0.7 copy.11
  81.1 0.8 copy.12
  81.9 0.6 copy.13

commit v7 on v6

--- a/solution.py
+++ b/solution.py
@@ -242,13 +242,15 @@
     for bit in range(bits):
         across(yt, bit, 3 + bit, NT)
 
+    exchange(F_OUT, yt, xr, 0, nt // 2)
+
     wait_bytes(recv.at[DZ], d2)
     wait_bytes(recv.at[MZ], m2)
     for i in range(1, NX):
         x = lax.rem(mex + i, NX)
         remote(d2, d3.at[mex], DX + i, tok=mehi * NX + x).start()
         remote(m2.at[:, :, x], m3.at[mex], MX + i, tok=mehi * NX + x).start()
-    exchange(F_OUT, yt, xr)
+    exchange(F_OUT, yt, xr, nt // 2, nt)
 
     rank = lax.broadcasted_iota(jnp.int32, (npool, BLK), 0)
     for i in range(NX):

time: 82.6 us -> 83.4 us (level)
  no operation moved by 1% of the time
where the time goes in v7:
time: 83.4 us; the launch traced here: 83.3 us
  Pallas kernels  80.6 us (97%)
  local copies, waits for them, and re-layouts  2.06 us (2%)
    pallas_call x1, Pallas kernels, shards(): pl.pallas_call(functools.partial(kernel, nt, ntp, ny), out_shape=(jax.Sha...  80.6 us
    unnamed x3, local copies, waits for them, and re-layouts  2.06 us

profile of v7, /device:TPU:1, one launch (start us, length us, event | category | flops | bytes accessed | tf_op | source)
XLA Modules:
  0.0 83.3 jit_solution(4084100854335447586)
XLA Ops:
  0.6 80.6 %shard_map.76 = (bf16[128,512]{1,0:T(8,128)(2,1)S(1)}, bf16[1024,256]{1,0:T(8,128)(2,1)S(1)}, f32[16,256]{1,0:T(8,128)S(1)}) custom-call(bf16[1024,256]{1,0:T(8,128)(2,1)} %tokens_h.1, bf16[10,2,2,128,128]{4,3,2,1,0:T(8,128)(2,1)} %mixw_h.1, bf16[256,2048]{1,0:T(8,128)(2,1)} %pw_h.1, s32[8,1,128]{2,1,0:T(1,128)} %bitcast.1, bf16[128,512]{1,0:T(8,128)(2,1)} %cot_h.1), custom_call_target="tpu_custom_call" | custom-call | tf_op jit(solution)/shard_map/pallas_call | solution.py:363
  81.2 0.7 copy.11
  81.9 0.8 copy.12
  82.7 0.6 copy.13
